TPU v7x, 32 devices: a whole 2x2x4 slice. The times are simulated.
32 devices in a mesh: fsdp: 32 (over z, y, x, core).
Axes of the slice: x: 2, y: 2, z: 4, core: 2. Of those that a mesh axis runs over, the one named last changes fastest.
Arguments:
- block_in: bfloat16 [64, 101, 768], P('fsdp'), may hold values from -6 to 6
- out_grad: bfloat16 [64, 101, 768], P('fsdp'), may hold values from -6 to 6
- image_counts: int32 [32], P('fsdp'), may hold values from 1 to 2, as said below
- ln1_gain: bfloat16 [768], P('fsdp'), may hold values from 0.5 to 1.5
- ln1_bias: bfloat16 [768], P('fsdp'), may hold values from -1.75 to 1.75
- w_qkv: bfloat16 [768, 2304], P('fsdp'), may hold values from -0.21875 to 0.21875
- q_bias: bfloat16 [768], P('fsdp'), may hold values from -3 to 3
- v_bias: bfloat16 [768], P('fsdp'), may hold values from -3 to 3
- w_out: bfloat16 [768, 768], P(None, 'fsdp'), may hold values from -1.75 to 1.75
- out_bias: bfloat16 [768], P('fsdp'), may hold values from -3 to 3
- ln2_gain: bfloat16 [768], P('fsdp'), may hold values from 0.5 to 1.5
- ln2_bias: bfloat16 [768], P('fsdp'), may hold values from -1.75 to 1.75
- w_up: bfloat16 [768, 3072], P('fsdp'), may hold values from -0.21875 to 0.21875
- up_bias: bfloat16 [3072], P('fsdp'), may hold values from -3 to 3
- w_down: bfloat16 [3072, 768], P(None, 'fsdp'), may hold values from -0.109375 to 0.109375
- down_bias: bfloat16 [768], P('fsdp'), may hold values from -3 to 3
Outputs:
- block_out: bfloat16 [64, 101, 768], P('fsdp')
- in_grad: bfloat16 [64, 101, 768], P('fsdp')
- grad_ln1_gain: float32 [768], P('fsdp')
- grad_ln1_bias: float32 [768], P('fsdp')
- grad_w_qkv: float32 [768, 2304], P('fsdp')
- grad_q_bias: float32 [768], P('fsdp')
- grad_v_bias: float32 [768], P('fsdp')
- grad_w_out: float32 [768, 768], P(None, 'fsdp')
- grad_out_bias: float32 [768], P('fsdp')
- grad_ln2_gain: float32 [768], P('fsdp')
- grad_ln2_bias: float32 [768], P('fsdp')
- grad_w_up: float32 [768, 3072], P('fsdp')
- grad_up_bias: float32 [3072], P('fsdp')
- grad_w_down: float32 [3072, 768], P(None, 'fsdp')
- grad_down_bias: float32 [768], P('fsdp')
Inputs may be any that keep to these rules, and one draw needn't show every extreme that they name: `image_counts`: every device holds at least one live image; some device holds 2.
All inputs are finite; a program needn't handle non-finite values.
Results may differ from a plain program's by a relative error of at most 0.014.
Values may be sent and summed in bfloat16 or wider, within the bound.
A program may use at most 192 MiB of HBM per device.

v0:
```python
import math

import jax
import jax.numpy as jnp
from jax import lax
from jax.sharding import PartitionSpec as P

HEAD_DIM = 64


NORM_EPS = 1e-06
INV_ROOT_TWO = 0.7071067811865476
INV_ROOT_TAU = 0.3989422804014327


def as_sent(value):

    def short(part):
        return part.astype(jnp.bfloat16) if part.dtype == jnp.float32 else part

    return jax.tree.map(short, value)


def swapped(value, axis, stride):
    return lax.ppermute(value, axis, [(i, i ^ 1 << stride) for i in range(lax.axis_size(axis))])


def mixing(form, left, right):
    return jnp.einsum(form, left, right, preferred_element_type=jnp.float32)


def norm_forward(stream, gain_row, offset):
    center = stream - jnp.mean(stream, axis=-1, keepdims=True)
    spread = lax.rsqrt(jnp.mean(center * center, axis=-1, keepdims=True) + NORM_EPS)
    scaled = center * spread
    return (scaled * gain_row + offset, scaled, spread)


def norm_backward(upstream, scaled, spread, gain_row):
    weighted = upstream * gain_row
    return spread * (
        weighted
        - jnp.mean(weighted, axis=-1, keepdims=True)
        - scaled * jnp.mean(weighted * scaled, axis=-1, keepdims=True)
    )


def gelu_value(pre_act):
    return 0.5 * pre_act * (1.0 + lax.erf(pre_act * INV_ROOT_TWO))


def gelu_slope(pre_act):
    return (
        0.5 * (1.0 + lax.erf(pre_act * INV_ROOT_TWO))
        + pre_act * jnp.exp(-0.5 * pre_act * pre_act) * INV_ROOT_TAU
    )


def forward(pictures, params):
    (
        ln1_gain,
        ln1_bias,
        w_qkv,
        q_bias,
        v_bias,
        w_out,
        out_bias,
        ln2_gain,
        ln2_bias,
        w_up,
        up_bias,
        w_down,
        down_bias,
    ) = params
    slots, seq_len, model_width = pictures.shape
    row_count = slots * seq_len
    head_count = model_width // HEAD_DIM
    query_scale = 1.0 / math.sqrt(HEAD_DIM)
    head_shape = (slots, seq_len, head_count, HEAD_DIM)
    residual = pictures.reshape(row_count, model_width).astype(jnp.float32)
    normed_f, scaled1, spread1 = norm_forward(
        residual, ln1_gain.astype(jnp.float32), ln1_bias.astype(jnp.float32)
    )
    normed1 = normed_f.astype(jnp.bfloat16)
    projected = jnp.dot(normed1, w_qkv, preferred_element_type=jnp.float32)
    queries = ((projected[:, :model_width] + q_bias.astype(jnp.float32)) * query_scale).astype(
        jnp.bfloat16
    )
    key_rows = projected[:, model_width : 2 * model_width].astype(jnp.bfloat16)
    value_rows = (projected[:, 2 * model_width :] + v_bias.astype(jnp.float32)).astype(jnp.bfloat16)
    scores = mixing("bqhd,bkhd->bhqk", queries.reshape(head_shape), key_rows.reshape(head_shape))
    log_total = jax.nn.logsumexp(scores, axis=-1)
    attn_probs = jnp.exp(scores - log_total[..., None]).astype(jnp.bfloat16)
    attended = (
        mixing("bhqk,bkhd->bqhd", attn_probs, value_rows.reshape(head_shape))
        .reshape(row_count, model_width)
        .astype(jnp.bfloat16)
    )
    stream = (
        residual
        + jnp.dot(attended, w_out, preferred_element_type=jnp.float32)
        + out_bias.astype(jnp.float32)
    )
    normed_g, scaled2, spread2 = norm_forward(
        stream, ln2_gain.astype(jnp.float32), ln2_bias.astype(jnp.float32)
    )
    normed2 = normed_g.astype(jnp.bfloat16)
    pre_act = jnp.dot(normed2, w_up, preferred_element_type=jnp.float32) + up_bias.astype(
        jnp.float32
    )
    activated = gelu_value(pre_act).astype(jnp.bfloat16)
    block_out = (
        stream
        + jnp.dot(activated, w_down, preferred_element_type=jnp.float32)
        + down_bias.astype(jnp.float32)
    ).astype(jnp.bfloat16)
    stashed = (
        normed1,
        scaled1,
        spread1,
        queries,
        key_rows,
        value_rows,
        log_total,
        attended,
        scaled2,
        spread2,
        normed2,
        pre_act,
        activated,
    )
    return (block_out.reshape(slots, seq_len, model_width), stashed)


def backward(out_grad, params, stashed):
    (
        ln1_gain,
        ln1_bias,
        w_qkv,
        q_bias,
        v_bias,
        w_out,
        out_bias,
        ln2_gain,
        ln2_bias,
        w_up,
        up_bias,
        w_down,
        down_bias,
    ) = params
    (
        normed1,
        scaled1,
        spread1,
        queries,
        key_rows,
        value_rows,
        log_total,
        attended,
        scaled2,
        spread2,
        normed2,
        pre_act,
        activated,
    ) = stashed
    slots, seq_len, model_width = out_grad.shape
    row_count = slots * seq_len
    head_count = model_width // HEAD_DIM
    query_scale = 1.0 / math.sqrt(HEAD_DIM)
    head_shape = (slots, seq_len, head_count, HEAD_DIM)
    grad_rows = out_grad.reshape(row_count, model_width)
    cotangent = grad_rows.astype(jnp.float32)
    grad_down_bias = jnp.sum(cotangent, axis=0)
    grad_w_down = jnp.dot(activated.T, grad_rows, preferred_element_type=jnp.float32)
    pre_grad = jnp.dot(grad_rows, w_down.T, preferred_element_type=jnp.float32) * gelu_slope(
        pre_act
    )
    pre_grad_b = pre_grad.astype(jnp.bfloat16)
    grad_up_bias = jnp.sum(pre_grad, axis=0)
    grad_w_up = jnp.dot(normed2.T, pre_grad_b, preferred_element_type=jnp.float32)
    normed2_grad = jnp.dot(pre_grad_b, w_up.T, preferred_element_type=jnp.float32)
    grad_ln2_gain = jnp.sum(normed2_grad * scaled2, axis=0)
    grad_ln2_bias = jnp.sum(normed2_grad, axis=0)
    stream_grad = cotangent + norm_backward(
        normed2_grad, scaled2, spread2, ln2_gain.astype(jnp.float32)
    )
    stream_grad_b = stream_grad.astype(jnp.bfloat16)
    grad_out_bias = jnp.sum(stream_grad, axis=0)
    grad_w_out = jnp.dot(attended.T, stream_grad_b, preferred_element_type=jnp.float32)
    attended_grad = (
        jnp.dot(stream_grad_b, w_out.T, preferred_element_type=jnp.float32)
        .astype(jnp.bfloat16)
        .reshape(head_shape)
    )
    query_heads = queries.reshape(head_shape)
    key_heads = key_rows.reshape(head_shape)
    value_heads = value_rows.reshape(head_shape)
    scores = mixing("bqhd,bkhd->bhqk", query_heads, key_heads)
    attn_probs = jnp.exp(scores - log_total[..., None])
    prob_grad = mixing("bqhd,bkhd->bhqk", attended_grad, value_heads)
    row_delta = jnp.sum(attn_probs * prob_grad, axis=-1, keepdims=True)
    score_grad = (attn_probs * (prob_grad - row_delta)).astype(jnp.bfloat16)
    value_grad = mixing("bhqk,bqhd->bkhd", attn_probs.astype(jnp.bfloat16), attended_grad).reshape(
        row_count, model_width
    )
    query_grad = (
        mixing("bhqk,bkhd->bqhd", score_grad, key_heads).reshape(row_count, model_width)
        * query_scale
    )
    key_grad = mixing("bhqk,bqhd->bkhd", score_grad, query_heads).reshape(row_count, model_width)
    grad_q_bias = jnp.sum(query_grad, axis=0)
    grad_v_bias = jnp.sum(value_grad, axis=0)
    qkv_grad = jnp.concatenate([query_grad, key_grad, value_grad], axis=1).astype(jnp.bfloat16)
    grad_w_qkv = jnp.dot(normed1.T, qkv_grad, preferred_element_type=jnp.float32)
    normed1_grad = jnp.dot(qkv_grad, w_qkv.T, preferred_element_type=jnp.float32)
    grad_ln1_gain = jnp.sum(normed1_grad * scaled1, axis=0)
    grad_ln1_bias = jnp.sum(normed1_grad, axis=0)
    in_grad = (
        stream_grad + norm_backward(normed1_grad, scaled1, spread1, ln1_gain.astype(jnp.float32))
    ).astype(jnp.bfloat16)
    return (
        in_grad.reshape(slots, seq_len, model_width),
        (
            grad_ln1_gain,
            grad_ln1_bias,
            grad_w_qkv,
            grad_q_bias,
            grad_v_bias,
            grad_w_out,
            grad_out_bias,
            grad_ln2_gain,
            grad_ln2_bias,
            grad_w_up,
            grad_up_bias,
            grad_w_down,
            grad_down_bias,
        ),
    )


def halving_sum(partial_value, shard_dims):
    bit_total = lax.axis_size("fsdp").bit_length() - 1
    own_index = lax.axis_index("fsdp")
    for bit_number in range(bit_total - 1, -1, -1):
        upper_bit = own_index >> bit_number & 1
        kept_parts = []
        sent_parts = []
        for member, axis_dim in zip(partial_value, shard_dims):
            half_len = member.shape[axis_dim] // 2
            kept_parts.append(
                lax.dynamic_slice_in_dim(member, upper_bit * half_len, half_len, axis_dim)
            )
            sent_parts.append(
                lax.dynamic_slice_in_dim(member, (1 - upper_bit) * half_len, half_len, axis_dim)
            )
        arrived = swapped(
            (
                as_sent(sent_parts[0]),
                as_sent(sent_parts[1]),
                as_sent(sent_parts[2]),
                as_sent(sent_parts[3]),
                as_sent(sent_parts[4]),
                as_sent(sent_parts[5]),
                as_sent(sent_parts[6]),
                as_sent(sent_parts[7]),
                as_sent(sent_parts[8]),
                as_sent(sent_parts[9]),
                as_sent(sent_parts[10]),
                as_sent(sent_parts[11]),
                as_sent(sent_parts[12]),
            ),
            "fsdp",
            bit_number,
        )
        partial_value = tuple((kept + incoming for kept, incoming in zip(kept_parts, arrived)))
    return partial_value


def body(
    block_in,
    out_grad,
    image_counts,
    ln1_gain,
    ln1_bias,
    w_qkv,
    q_bias,
    v_bias,
    w_out,
    out_bias,
    ln2_gain,
    ln2_bias,
    w_up,
    up_bias,
    w_down,
    down_bias,
):
    held_count = image_counts[0]
    slot_count = block_in.shape[0]
    shard_dims = (0, 0, 0, 0, 0, 1, 0, 0, 0, 0, 0, 1, 0)
    gathered = (
        lax.all_gather(ln1_gain, "fsdp", axis=0, tiled=True),
        lax.all_gather(ln1_bias, "fsdp", axis=0, tiled=True),
        lax.all_gather(w_qkv, "fsdp", axis=0, tiled=True),
        lax.all_gather(q_bias, "fsdp", axis=0, tiled=True),
        lax.all_gather(v_bias, "fsdp", axis=0, tiled=True),
        lax.all_gather(w_out, "fsdp", axis=1, tiled=True),
        lax.all_gather(out_bias, "fsdp", axis=0, tiled=True),
        lax.all_gather(ln2_gain, "fsdp", axis=0, tiled=True),
        lax.all_gather(ln2_bias, "fsdp", axis=0, tiled=True),
        lax.all_gather(w_up, "fsdp", axis=0, tiled=True),
        lax.all_gather(up_bias, "fsdp", axis=0, tiled=True),
        lax.all_gather(w_down, "fsdp", axis=1, tiled=True),
        lax.all_gather(down_bias, "fsdp", axis=0, tiled=True),
    )
    live_slots = (jnp.arange(slot_count, dtype=jnp.int32) < held_count)[:, None, None]
    result, stashed = forward(block_in, gathered)
    masked_grad = jnp.where(live_slots, out_grad, jnp.zeros_like(out_grad))
    for_back = (
        lax.all_gather(ln1_gain, "fsdp", axis=0, tiled=True),
        lax.all_gather(ln1_bias, "fsdp", axis=0, tiled=True),
        lax.all_gather(w_qkv, "fsdp", axis=0, tiled=True),
        lax.all_gather(q_bias, "fsdp", axis=0, tiled=True),
        lax.all_gather(v_bias, "fsdp", axis=0, tiled=True),
        lax.all_gather(w_out, "fsdp", axis=1, tiled=True),
        lax.all_gather(out_bias, "fsdp", axis=0, tiled=True),
        lax.all_gather(ln2_gain, "fsdp", axis=0, tiled=True),
        lax.all_gather(ln2_bias, "fsdp", axis=0, tiled=True),
        lax.all_gather(w_up, "fsdp", axis=0, tiled=True),
        lax.all_gather(up_bias, "fsdp", axis=0, tiled=True),
        lax.all_gather(w_down, "fsdp", axis=1, tiled=True),
        lax.all_gather(down_bias, "fsdp", axis=0, tiled=True),
    )
    back_rows, grad_terms = backward(masked_grad, for_back, stashed)
    totals = halving_sum(grad_terms, shard_dims)
    block_out = jnp.where(live_slots, result, jnp.zeros_like(result))
    in_grad = jnp.where(live_slots, back_rows, jnp.zeros_like(back_rows))
    return (block_out, in_grad) + tuple(totals)


def solution(mesh):
    return jax.shard_map(
        body,
        mesh=mesh,
        in_specs=(
            P("fsdp", None, None),
            P("fsdp", None, None),
            P("fsdp"),
            P("fsdp"),
            P("fsdp"),
            P("fsdp", None),
            P("fsdp"),
            P("fsdp"),
            P(None, "fsdp"),
            P("fsdp"),
            P("fsdp"),
            P("fsdp"),
            P("fsdp", None),
            P("fsdp"),
            P(None, "fsdp"),
            P("fsdp"),
        ),
        out_specs=(
            P("fsdp", None, None),
            P("fsdp", None, None),
            P("fsdp"),
            P("fsdp"),
            P("fsdp", None),
            P("fsdp"),
            P("fsdp"),
            P(None, "fsdp"),
            P("fsdp"),
            P("fsdp"),
            P("fsdp"),
            P("fsdp", None),
            P("fsdp"),
            P(None, "fsdp"),
            P("fsdp"),
        ),
        check_vma=False,
    )
```

profile of v0, /device:TPU:0, one launch (start us, length us, event | category | flops | bytes accessed | tf_op | source)
XLA Modules:
  0.0 772.6 jit_solution(13443814528058108558)
XLA Ops:
  11.9 4.1 collective-permute-start.60
  23.5 41.2 %all-reduce.9 = (bf16[768]{0:T(1024)(128)(2,1)S(1)}, bf16[768]{0:T(1024)(128)(2,1)S(1)}, bf16[768]{0:T(1024)(128)(2,1)S(1)}, bf16[768]{0:T(1024)(128)(2,1)S(1)},...) all-reduce(bf16[768]{0:T(1024)(128)(2,1)S(1)} %dynamic-update-slice, ...), channel_id=1, replica_groups=mesh['fsdp'=32] {'fsdp'}, use_global_device_ids=true, to_apply=%add.1 | all-reduce | flops 9216 | bytes 36864
  70.0 2.8 collective-permute-done.61
  73.0 2.3 collective-permute-start.62
  77.0 2.0 collective-permute-start.63
  82.4 3.0 fusion.23
  90.9 39.3 %all-gather.7.cloned.1.call-done = bf16[768,768]{0,1:T(8,128)(2,1)} async-done(((bf16[768,24]{0,1:T(8,128)(2,1)}), bf16[768,768]{0,1:T(8,128)(2,1)}) %all-gather.7.cloned.1.call-update) | async-done | bytes 1179664 | tf_op jit(solution)/shard_map/all_gather | solution.py:306
  130.1 1.9 fusion.28
  132.3 63.3 %all-gather.9.cloned.1.call-done = bf16[768,3072]{1,0:T(8,128)(2,1)} async-done(((bf16[24,3072]{1,0:T(8,128)(2,1)}), bf16[768,3072]{1,0:T(8,128)(2,1)}) %all-gather.9.cloned.1.call-update) | async-done | bytes 4718608 | tf_op jit(solution)/shard_map/all_gather | solution.py:310
  195.6 5.8 multiply_convert_fusion
  201.4 58.9 %all-gather.11.cloned.1.call-done = bf16[3072,768]{0,1:T(8,128)(2,1)} async-done(((bf16[3072,24]{0,1:T(8,128)(2,1)}), bf16[3072,768]{0,1:T(8,128)(2,1)}) %all-gather.11.cloned.1.call-update) | async-done | bytes 4718608 | tf_op jit(solution)/shard_map/all_gather | solution.py:312
  260.3 6.5 fusion.29
  266.8 2.4 multiply_reduce_fusion.1
  271.6 2.3 reshape.189
  274.0 2.5 copy.112
  282.8 1.9 fusion.19
  284.8 5.2 fusion.13
  292.4 2.2 copy.119
  294.5 2.0 reshape.164
  296.5 2.2 copy.122
  298.7 2.0 reshape.165
  302.8 4.2 fusion.22
  310.6 5.0 fusion.30
  315.6 4.0 fusion.6
  325.0 3.4 dynamic-slice_convert_fusion.2
  333.2 2.8 dynamic-slice_convert_fusion.1
  336.1 3.2 dynamic-slice_convert_fusion
  342.8 78.5 %collective-permute-done.15 = bf16[384]{0:T(512)(128)(2,1)S(1)} collective-permute-done((bf16[384]{0:T(512)(128)(2,1)S(1)}, bf16[384]{0:T(512)(128)(2,1)S(1)}, u32[]{:S(2)}, u32[]{:S(2)}) %collective-permute-start.15) | collective-permute-done | bytes 800 | tf_op jit(solution)/shard_map/ppermute | solution.py:25
  421.4 2.9 collective-permute-start.40
  424.4 8.7 %collective-permute-done.30 = bf16[384]{0:T(512)(128)(2,1)S(1)} collective-permute-done((bf16[384]{0:T(512)(128)(2,1)S(1)}, bf16[384]{0:T(512)(128)(2,1)S(1)}, u32[]{:S(2)}, u32[]{:S(2)}) %collective-permute-start.30) | collective-permute-done | bytes 800 | tf_op jit(solution)/shard_map/ppermute | solution.py:25
  433.2 2.9 collective-permute-start.50
  436.8 46.5 %collective-permute-done.1 = bf16[192]{0:T(256)(128)(2,1)S(1)} collective-permute-done((bf16[192]{0:T(256)(128)(2,1)S(1)}, bf16[192]{0:T(256)(128)(2,1)S(1)}, u32[]{:S(2)}, u32[]{:S(2)}) %collective-permute-start.1) | collective-permute-done | bytes 416 | tf_op jit(solution)/shard_map/ppermute | solution.py:25
  483.4 2.4 collective-permute-start.6
  487.4 2.0 collective-permute-start.16
  491.0 2.0 collective-permute-start.21
  494.6 2.0 collective-permute-start.31
  498.1 2.0 collective-permute-start.36
  501.7 2.0 collective-permute-start.41
  510.4 2.0 collective-permute-done.7
  514.0 2.0 collective-permute-done.17
  517.5 2.0 collective-permute-done.22
  521.1 2.0 collective-permute-done.32
  524.9 1.8 collective-permute-done.37
  528.5 1.8 collective-permute-done.42
  531.9 2.0 collective-permute-done.3
  535.4 2.0 collective-permute-done.8
  539.0 2.0 collective-permute-done.18
  542.6 2.0 collective-permute-done.23
  546.1 2.0 collective-permute-done.33
  549.7 2.0 collective-permute-done.38
  553.3 2.0 collective-permute-done.43
  562.2 2.1 collective-permute-start.55
  567.9 48.1 %collective-permute-done.51 = bf16[768]{0:T(1024)(128)(2,1)S(1)} collective-permute-done((bf16[768]{0:T(1024)(128)(2,1)S(1)}, bf16[768]{0:T(1024)(128)(2,1)S(1)}, u32[]{:S(2)}, u32[]{:S(2)}) %collective-permute-start.51) | collective-permute-done | bytes 1568 | tf_op jit(solution)/shard_map/ppermute | solution.py:25
  617.7 3.9 collective-permute-done.26
  623.9 3.0 collective-permute-done.27
  630.3 2.5 collective-permute-start.11
  635.4 50.5 %collective-permute-done.11 = bf16[192,2304]{1,0:T(8,128)(2,1)S(1)} collective-permute-done((bf16[192,2304]{1,0:T(8,128)(2,1)S(1)}, bf16[192,2304]{1,0:T(8,128)(2,1)S(1)}, u32[]{:S(2)}, u32[]{:S(2)}) %collective-permute-start.11) | collective-permute-done | bytes 884768 | tf_op jit(solution)/shard_map/ppermute | solution.py:25
  689.0 9.4 %collective-permute-done.12 = bf16[96,2304]{1,0:T(8,128)(2,1)S(1)} collective-permute-done((bf16[96,2304]{1,0:T(8,128)(2,1)S(1)}, bf16[96,2304]{1,0:T(8,128)(2,1)S(1)}, u32[]{:S(2)}, u32[]{:S(2)}) %collective-permute-start.12) | collective-permute-done | bytes 442400 | tf_op jit(solution)/shard_map/ppermute | solution.py:25
  700.0 2.3 convert_add_fusion
  702.3 2.7 collective-permute-done.13
  707.2 10.6 %collective-permute-done.46 = bf16[192,3072]{1,0:T(8,128)(2,1)S(1)} collective-permute-done((bf16[192,3072]{1,0:T(8,128)(2,1)S(1)}, bf16[192,3072]{1,0:T(8,128)(2,1)S(1)}, u32[]{:S(2)}, u32[]{:S(2)}) %collective-permute-start.46) | collective-permute-done | bytes 1179680 | tf_op jit(solution)/shard_map/ppermute | solution.py:25
  718.8 23.1 %collective-permute-done.56 = bf16[3072,192]{0,1:T(8,128)(2,1)S(1)} collective-permute-done((bf16[3072,192]{0,1:T(8,128)(2,1)S(1)}, bf16[3072,192]{0,1:T(8,128)(2,1)S(1)}, u32[]{:S(2)}, u32[]{:S(2)}) %collective-permute-start.56) | collective-permute-done | bytes 1179680 | tf_op jit(solution)/shard_map/ppermute | solution.py:25
  744.6 11.9 %collective-permute-done.57 = bf16[3072,96]{0,1:T(8,128)(2,1)S(1)} collective-permute-done((bf16[3072,96]{0,1:T(8,128)(2,1)S(1)}, bf16[3072,96]{0,1:T(8,128)(2,1)S(1)}, u32[]{:S(2)}, u32[]{:S(2)}) %collective-permute-start.57) | collective-permute-done | bytes 589856 | tf_op jit(solution)/shard_map/ppermute | solution.py:25
  757.4 6.2 collective-permute-done.58
  (394 shorter events, 127.1 us)
Async XLA Ops:
  7.2 75.2 %all-gather.5.cloned.1.call-start = ((), (), s32[]{:S(2)}) async-start(), calls=%async_computation | async-start | bytes 3649536 | tf_op jit(solution)/shard_map/all_gather | solution.py:303
  7.9 122.2 %all-gather.7.cloned.1.call-start = ((), (), s32[]{:S(2)}) async-start(), calls=%async_computation.1 | async-start | bytes 1216512 | tf_op jit(solution)/shard_map/all_gather | solution.py:306
  8.7 186.9 %all-gather.9.cloned.1.call-start = ((), (), s32[]{:S(2)}) async-start(), calls=%async_computation.2 | async-start | bytes 4866048 | tf_op jit(solution)/shard_map/all_gather | solution.py:310
  9.4 250.9 %all-gather.11.cloned.1.call-start = ((), (), s32[]{:S(2)}) async-start(), calls=%async_computation.3 | async-start | bytes 4866048 | tf_op jit(solution)/shard_map/all_gather | solution.py:312
  11.9 57.2 %collective-permute-start.60 = (bf16[384]{0:T(512)(128)(2,1)S(1)}, bf16[384]{0:T(512)(128)(2,1)S(1)}, u32[]{:S(2)}, u32[]{:S(2)}) collective-permute-start(bf16[384]{0:T(512)(128)(2,1)S(1)} %dynamic_slice.652), channel_id=1, source_target_pairs={{0,16},{1,17},{2,18},{3,19},{4,20},{5,21},{6,22},{7,23},{8,24},{9,... | collective-permute-start | bytes 2312 | tf_op jit(solution)/shard_map/ppermute | solution.py:25
  69.3 3.6 collective-permute-start.61
  73.0 3.8 collective-permute-start.62
  77.0 3.6 collective-permute-start.63
  80.7 1.2 collective-permute-start.64
  322.0 17.7 %collective-permute-start = (bf16[384]{0:T(512)(128)(2,1)S(1)}, bf16[384]{0:T(512)(128)(2,1)S(1)}, u32[]{:S(2)}, u32[]{:S(2)}) collective-permute-start(bf16[384]{0:T(512)(128)(2,1)S(1)} %dynamic_slice.660), channel_id=1, source_target_pairs={{0,16},{1,17},{2,18},{3,19},{4,20},{5,21},{6,22},{7,23},{8,24},{9,... | collective-permute-start | bytes 2312 | tf_op jit(solution)/shard_map/ppermute | solution.py:25
  323.7 17.4 %collective-permute-start.5 = (bf16[384]{0:T(512)(128)(2,1)S(1)}, bf16[384]{0:T(512)(128)(2,1)S(1)}, u32[]{:S(2)}, u32[]{:S(2)}) collective-permute-start(bf16[384]{0:T(512)(128)(2,1)S(1)} %dynamic_slice.659), channel_id=1, source_target_pairs={{0,16},{1,17},{2,18},{3,19},{4,20},{5,21},{6,22},{7,23},{8,24},{9,... | collective-permute-start | bytes 2312 | tf_op jit(solution)/shard_map/ppermute | solution.py:25
  328.4 300.1 %collective-permute-start.10 = (bf16[384,2304]{1,0:T(8,128)(2,1)}, bf16[384,2304]{1,0:T(8,128)(2,1)}, u32[]{:S(2)}, u32[]{:S(2)}) collective-permute-start(bf16[384,2304]{1,0:T(8,128)(2,1)} %dynamic-slice_convert_fusion.2), channel_id=1, source_target_pairs={{0,16},{1,17},{2,18},{3,19},{4,20},{5,21},{6,22},{7,23},{8,24},{9,... | collective-permute-start | bytes 5308424 | tf_op jit(solution)/shard_map/ppermute | solution.py:25
  330.2 91.2 %collective-permute-start.15 = (bf16[384]{0:T(512)(128)(2,1)S(1)}, bf16[384]{0:T(512)(128)(2,1)S(1)}, u32[]{:S(2)}, u32[]{:S(2)}) collective-permute-start(bf16[384]{0:T(512)(128)(2,1)S(1)} %dynamic_slice.658), channel_id=1, source_target_pairs={{0,16},{1,17},{2,18},{3,19},{4,20},{5,21},{6,22},{7,23},{8,24},{9,... | collective-permute-start | bytes 2312 | tf_op jit(solution)/shard_map/ppermute | solution.py:25
  331.6 89.8 %collective-permute-start.20 = (bf16[384]{0:T(512)(128)(2,1)S(1)}, bf16[384]{0:T(512)(128)(2,1)S(1)}, u32[]{:S(2)}, u32[]{:S(2)}) collective-permute-start(bf16[384]{0:T(512)(128)(2,1)S(1)} %dynamic_slice.657), channel_id=1, source_target_pairs={{0,16},{1,17},{2,18},{3,19},{4,20},{5,21},{6,22},{7,23},{8,24},{9,... | collective-permute-start | bytes 2312 | tf_op jit(solution)/shard_map/ppermute | solution.py:25
  339.7 225.3 %collective-permute-start.25 = (bf16[768,384]{0,1:T(8,128)(2,1)S(1)}, bf16[768,384]{0,1:T(8,128)(2,1)S(1)}, u32[]{:S(2)}, u32[]{:S(2)}) collective-permute-start(bf16[768,384]{0,1:T(8,128)(2,1)S(1)} %dynamic-slice_convert_fusion.8), channel_id=1, source_target_pairs={{0,16},{1,17},{2,18},{3,19},{4,20},{5,21},{6,22},{7,23},{8,24},{9,... | collective-permute-start | bytes 1769480 | tf_op jit(solution)/shard_map/ppermute | solution.py:25
  341.1 92.0 %collective-permute-start.30 = (bf16[384]{0:T(512)(128)(2,1)S(1)}, bf16[384]{0:T(512)(128)(2,1)S(1)}, u32[]{:S(2)}, u32[]{:S(2)}) collective-permute-start(bf16[384]{0:T(512)(128)(2,1)S(1)} %dynamic_slice.656), channel_id=1, source_target_pairs={{0,16},{1,17},{2,18},{3,19},{4,20},{5,21},{6,22},{7,23},{8,24},{9,... | collective-permute-start | bytes 2312 | tf_op jit(solution)/shard_map/ppermute | solution.py:25
  421.3 11.9 %collective-permute-start.35 = (bf16[384]{0:T(512)(128)(2,1)S(1)}, bf16[384]{0:T(512)(128)(2,1)S(1)}, u32[]{:S(2)}, u32[]{:S(2)}) collective-permute-start(bf16[384]{0:T(512)(128)(2,1)S(1)} %dynamic_slice.655), channel_id=1, source_target_pairs={{0,16},{1,17},{2,18},{3,19},{4,20},{5,21},{6,22},{7,23},{8,24},{9,... | collective-permute-start | bytes 2312 | tf_op jit(solution)/shard_map/ppermute | solution.py:25
  421.4 14.9 %collective-permute-start.40 = (bf16[384]{0:T(512)(128)(2,1)S(1)}, bf16[384]{0:T(512)(128)(2,1)S(1)}, u32[]{:S(2)}, u32[]{:S(2)}) collective-permute-start(bf16[384]{0:T(512)(128)(2,1)S(1)} %dynamic_slice.654), channel_id=1, source_target_pairs={{0,16},{1,17},{2,18},{3,19},{4,20},{5,21},{6,22},{7,23},{8,24},{9,... | collective-permute-start | bytes 2312 | tf_op jit(solution)/shard_map/ppermute | solution.py:25
  433.1 254.6 %collective-permute-start.45 = (bf16[384,3072]{1,0:T(8,128)(2,1)S(1)}, bf16[384,3072]{1,0:T(8,128)(2,1)S(1)}, u32[]{:S(2)}, u32[]{:S(2)}) collective-permute-start(bf16[384,3072]{1,0:T(8,128)(2,1)S(1)} %dynamic-slice_convert_fusion.1), channel_id=1, source_target_pairs={{0,16},{1,17},{2,18},{3,19},{4,20},{5,21},{6,22},{7,23},{8,24},{9,... | collective-permute-start | bytes 7077896 | tf_op jit(solution)/shard_map/ppermute | solution.py:25
  433.2 131.7 %collective-permute-start.50 = (bf16[1536]{0:T(1024)(128)(2,1)S(1)}, bf16[1536]{0:T(1024)(128)(2,1)S(1)}, u32[]{:S(2)}, u32[]{:S(2)}) collective-permute-start(bf16[1536]{0:T(1024)(128)(2,1)S(1)} %dynamic_slice.650), channel_id=1, source_target_pairs={{0,16},{1,17},{2,18},{3,19},{4,20},{5,21},{6,22},{7,23},{8,24},{9,... | collective-permute-start | bytes 9224 | tf_op jit(solution)/shard_map/ppermute | solution.py:25
  436.3 47.1 %collective-permute-start.1 = (bf16[192]{0:T(256)(128)(2,1)S(1)}, bf16[192]{0:T(256)(128)(2,1)S(1)}, u32[]{:S(2)}, u32[]{:S(2)}) collective-permute-start(bf16[192]{0:T(256)(128)(2,1)S(1)} %dynamic_slice.669), channel_id=1, source_target_pairs={{0,8},{1,9},{2,10},{3,11},{4,12},{5,13},{6,14},{7,15},{8,0},{9,1},... | collective-permute-start | bytes 1160 | tf_op jit(solution)/shard_map/ppermute | solution.py:25
  483.4 4.1 collective-permute-start.6
  487.4 3.6 collective-permute-start.16
  491.0 3.6 collective-permute-start.21
  494.6 3.6 collective-permute-start.31
  498.1 3.6 collective-permute-start.36
  501.7 3.6 collective-permute-start.41
  505.3 3.6 collective-permute-start.2
  508.8 3.6 collective-permute-start.7
  512.4 3.6 collective-permute-start.17
  516.0 3.6 collective-permute-start.22
  519.6 3.6 collective-permute-start.32
  523.1 3.6 collective-permute-start.37
  526.7 3.6 collective-permute-start.42
  530.3 3.6 collective-permute-start.3
  533.8 3.6 collective-permute-start.8
  537.4 3.6 collective-permute-start.18
  541.0 3.6 collective-permute-start.23
  544.5 3.6 collective-permute-start.33
  548.1 3.6 collective-permute-start.38
  551.7 3.6 collective-permute-start.43
  555.3 1.2 collective-permute-start.4
  562.2 137.8 %collective-permute-start.55 = (bf16[3072,384]{0,1:T(8,128)(2,1)S(1)}, bf16[3072,384]{0,1:T(8,128)(2,1)}, u32[]{:S(2)}, u32[]{:S(2)}) collective-permute-start(bf16[3072,384]{0,1:T(8,128)(2,1)S(1)} %dynamic-slice_convert_fusion), channel_id=1, source_target_pairs={{0,16},{1,17},{2,18},{3,19},{4,20},{5,21},{6,22},{7,23},{8,24},{9,... | collective-permute-start | bytes 7077896 | tf_op jit(solution)/shard_map/ppermute | solution.py:25
  564.9 1.2 collective-permute-start.44
  565.0 51.0 %collective-permute-start.51 = (bf16[768]{0:T(1024)(128)(2,1)S(1)}, bf16[768]{0:T(1024)(128)(2,1)S(1)}, u32[]{:S(2)}, u32[]{:S(2)}) collective-permute-start(bf16[768]{0:T(1024)(128)(2,1)S(1)} %dynamic_slice.651), channel_id=1, source_target_pairs={{0,8},{1,9},{2,10},{3,11},{4,12},{5,13},{6,14},{7,15},{8,0},{9,1},... | collective-permute-start | bytes 4616 | tf_op jit(solution)/shard_map/ppermute | solution.py:25
  566.0 55.5 %collective-permute-start.26 = (bf16[768,192]{0,1:T(8,128)(2,1)S(1)}, bf16[768,192]{0,1:T(8,128)(2,1)S(1)}, u32[]{:S(2)}, u32[]{:S(2)}) collective-permute-start(bf16[768,192]{0,1:T(8,128)(2,1)S(1)} %dynamic-slice_convert_fusion.12), channel_id=1, source_target_pairs={{0,8},{1,9},{2,10},{3,11},{4,12},{5,13},{6,14},{7,15},{8,0},{9,1},... | collective-permute-start | bytes 884744 | tf_op jit(solution)/shard_map/ppermute | solution.py:25
  616.2 7.0 collective-permute-start.52
  621.6 5.2 collective-permute-start.27
  623.3 9.5 %collective-permute-start.53 = (bf16[192]{0:T(256)(128)(2,1)S(1)}, bf16[192]{0:T(256)(128)(2,1)S(1)}, u32[]{:S(2)}, u32[]{:S(2)}) collective-permute-start(bf16[192]{0:T(256)(128)(2,1)S(1)} %dynamic_slice.662), channel_id=1, source_target_pairs={{0,2},{1,3},{2,0},{3,1},{4,6},{5,7},{6,4},{7,5},{8,10},{9,11},{10,... | collective-permute-start | bytes 1160 | tf_op jit(solution)/shard_map/ppermute | solution.py:25
  626.9 6.1 collective-permute-start.28
  630.3 55.6 %collective-permute-start.11 = (bf16[192,2304]{1,0:T(8,128)(2,1)S(1)}, bf16[192,2304]{1,0:T(8,128)(2,1)S(1)}, u32[]{:S(2)}, u32[]{:S(2)}) collective-permute-start(bf16[192,2304]{1,0:T(8,128)(2,1)S(1)} %dynamic-slice_convert_fusion.5), channel_id=1, source_target_pairs={{0,8},{1,9},{2,10},{3,11},{4,12},{5,13},{6,14},{7,15},{8,0},{9,1},... | collective-permute-start | bytes 2654216 | tf_op jit(solution)/shard_map/ppermute | solution.py:25
  633.0 1.2 collective-permute-start.54
  633.1 1.7 collective-permute-start.29
  686.2 12.2 %collective-permute-start.12 = (bf16[96,2304]{1,0:T(8,128)(2,1)S(1)}, bf16[96,2304]{1,0:T(8,128)(2,1)S(1)}, u32[]{:S(2)}, u32[]{:S(2)}) collective-permute-start(bf16[96,2304]{1,0:T(8,128)(2,1)S(1)} %dynamic-slice_convert_fusion.9), channel_id=1, source_target_pairs={{0,4},{1,5},{2,6},{3,7},{4,0},{5,1},{6,2},{7,3},{8,12},{9,13},{10,... | collective-permute-start | bytes 1327112 | tf_op jit(solution)/shard_map/ppermute | solution.py:25
  688.9 28.9 %collective-permute-start.46 = (bf16[192,3072]{1,0:T(8,128)(2,1)S(1)}, bf16[192,3072]{1,0:T(8,128)(2,1)S(1)}, u32[]{:S(2)}, u32[]{:S(2)}) collective-permute-start(bf16[192,3072]{1,0:T(8,128)(2,1)S(1)} %dynamic-slice_convert_fusion.4), channel_id=1, source_target_pairs={{0,8},{1,9},{2,10},{3,11},{4,12},{5,13},{6,14},{7,15},{8,0},{9,1},... | collective-permute-start | bytes 3538952 | tf_op jit(solution)/shard_map/ppermute | solution.py:25
  698.5 6.6 collective-permute-start.13
  705.1 1.4 collective-permute-start.14
  705.4 36.5 %collective-permute-start.56 = (bf16[3072,192]{0,1:T(8,128)(2,1)S(1)}, bf16[3072,192]{0,1:T(8,128)(2,1)S(1)}, u32[]{:S(2)}, u32[]{:S(2)}) collective-permute-start(bf16[3072,192]{0,1:T(8,128)(2,1)S(1)} %dynamic-slice_convert_fusion.3), channel_id=1, source_target_pairs={{0,8},{1,9},{2,10},{3,11},{4,12},{5,13},{6,14},{7,15},{8,0},{9,1},... | collective-permute-start | bytes 3538952 | tf_op jit(solution)/shard_map/ppermute | solution.py:25
  718.2 24.7 %collective-permute-start.47 = (bf16[96,3072]{1,0:T(8,128)(2,1)S(1)}, bf16[96,3072]{1,0:T(8,128)(2,1)S(1)}, u32[]{:S(2)}, u32[]{:S(2)}) collective-permute-start(bf16[96,3072]{1,0:T(8,128)(2,1)S(1)} %dynamic-slice_convert_fusion.7), channel_id=1, source_target_pairs={{0,4},{1,5},{2,6},{3,7},{4,0},{5,1},{6,2},{7,3},{8,12},{9,13},{10,... | collective-permute-start | bytes 1769480 | tf_op jit(solution)/shard_map/ppermute | solution.py:25
  742.3 14.2 %collective-permute-start.57 = (bf16[3072,96]{0,1:T(8,128)(2,1)S(1)}, bf16[3072,96]{0,1:T(8,128)(2,1)S(1)}, u32[]{:S(2)}, u32[]{:S(2)}) collective-permute-start(bf16[3072,96]{0,1:T(8,128)(2,1)S(1)} %dynamic-slice_convert_fusion.6), channel_id=1, source_target_pairs={{0,4},{1,5},{2,6},{3,7},{4,0},{5,1},{6,2},{7,3},{8,12},{9,13},{10,... | collective-permute-start | bytes 1769480 | tf_op jit(solution)/shard_map/ppermute | solution.py:25
  743.1 14.2 %collective-permute-start.48 = (bf16[48,3072]{1,0:T(8,128)(2,1)S(1)}, bf16[48,3072]{1,0:T(8,128)(2,1)S(1)}, u32[]{:S(2)}, u32[]{:S(2)}) collective-permute-start(bf16[48,3072]{1,0:T(8,128)(2,1)S(1)} %dynamic-slice_convert_fusion.11), channel_id=1, source_target_pairs={{0,2},{1,3},{2,0},{3,1},{4,6},{5,7},{6,4},{7,5},{8,10},{9,11},{10,... | collective-permute-start | bytes 884744 | tf_op jit(solution)/shard_map/ppermute | solution.py:25
  756.6 7.0 collective-permute-start.58
  757.4 6.5 collective-permute-start.49
  763.7 1.4 collective-permute-start.59
  (47 other events, 1676.0 us)
Sparse Core Ops, SparseCore 0:
  10.9 63.4 all-gather.4
  77.3 52.7 all-gather.6
  133.0 62.4 all-gather.8
  198.3 61.9 all-gather.10
where the time goes:
time: 781 us; the launch traced here: 773 us
  waiting for transfers between devices  516 us (66%)
  starting transfers between devices  77.4 us (10%)
  local copies, waits for them, and re-layouts  49.6 us (6%)
  matrix products  48.9 us (6%)
  blocking collectives  41.2 us (5%)
  other arithmetic  23.5 us (3%)
  between operations  15.7 us (2%)
    ppermute x65, waiting for transfers between devices, swapped(): lax.ppermute(value, axis, [(i, i ^ 1 << stride) for i in range(lax.axis_s...  352 us
    ppermute x65, starting transfers between devices, swapped(): lax.ppermute(value, axis, [(i, i ^ 1 << stride) for i in range(lax.axis_s...  77.3 us
    all_gather x1, waiting for transfers between devices, body(): lax.all_gather(w_up, 'fsdp', axis=0, tiled=True)  63.3 us
    all_gather x1, waiting for transfers between devices, body(): lax.all_gather(w_down, 'fsdp', axis=1, tiled=True)  58.9 us
    unnamed x1, blocking collectives  41.2 us
    all_gather x1, waiting for transfers between devices, body(): lax.all_gather(w_out, 'fsdp', axis=1, tiled=True)  39.3 us
    add x65, other arithmetic, halving_sum(): kept + incoming  17.3 us
  transfers between devices with their start and end apart: 69, of which 50 were waited for; matrix products, arithmetic and copies ran while one was open for 8% of the time, Pallas kernels for 0%

commit v1 on v0

--- a/solution.py
+++ b/solution.py
@@ -1,8 +1,11 @@
+import functools
 import math
 
 import jax
 import jax.numpy as jnp
 from jax import lax
+from jax.experimental import pallas as pl
+from jax.experimental.pallas import tpu as pltpu
 from jax.sharding import PartitionSpec as P
 
 HEAD_DIM = 64
@@ -13,20 +16,19 @@
 INV_ROOT_TAU = 0.3989422804014327
 
 
-def as_sent(value):
-
-    def short(part):
-        return part.astype(jnp.bfloat16) if part.dtype == jnp.float32 else part
-
-    return jax.tree.map(short, value)
-
-
-def swapped(value, axis, stride):
-    return lax.ppermute(value, axis, [(i, i ^ 1 << stride) for i in range(lax.axis_size(axis))])
-
-
 def mixing(form, left, right):
     return jnp.einsum(form, left, right, preferred_element_type=jnp.float32)
+
+
+def against(left, right):
+    return lax.dot_general(left, right, (((1,), (1,)), ((), ())), preferred_element_type=jnp.float32)
+
+
+def over_rows(left, right):
+    product = lax.dot_general(
+        left, right, (((0,), (0,)), ((), ())), preferred_element_type=jnp.float32
+    )
+    return product.astype(jnp.bfloat16)
 
 
 def norm_forward(stream, gain_row, offset):
@@ -98,7 +100,7 @@
     )
     stream = (
         residual
-        + jnp.dot(attended, w_out, preferred_element_type=jnp.float32)
+        + against(attended, w_out)
         + out_bias.astype(jnp.float32)
     )
     normed_g, scaled2, spread2 = norm_forward(
@@ -111,7 +113,7 @@
     activated = gelu_value(pre_act).astype(jnp.bfloat16)
     block_out = (
         stream
-        + jnp.dot(activated, w_down, preferred_element_type=jnp.float32)
+        + against(activated, w_down)
         + down_bias.astype(jnp.float32)
     ).astype(jnp.bfloat16)
     stashed = (
@@ -171,14 +173,14 @@
     grad_rows = out_grad.reshape(row_count, model_width)
     cotangent = grad_rows.astype(jnp.float32)
     grad_down_bias = jnp.sum(cotangent, axis=0)
-    grad_w_down = jnp.dot(activated.T, grad_rows, preferred_element_type=jnp.float32)
-    pre_grad = jnp.dot(grad_rows, w_down.T, preferred_element_type=jnp.float32) * gelu_slope(
+    grad_w_down = over_rows(grad_rows, activated)
+    pre_grad = jnp.dot(grad_rows, w_down, preferred_element_type=jnp.float32) * gelu_slope(
         pre_act
     )
     pre_grad_b = pre_grad.astype(jnp.bfloat16)
     grad_up_bias = jnp.sum(pre_grad, axis=0)
-    grad_w_up = jnp.dot(normed2.T, pre_grad_b, preferred_element_type=jnp.float32)
-    normed2_grad = jnp.dot(pre_grad_b, w_up.T, preferred_element_type=jnp.float32)
+    grad_w_up = over_rows(normed2, pre_grad_b)
+    normed2_grad = against(pre_grad_b, w_up)
     grad_ln2_gain = jnp.sum(normed2_grad * scaled2, axis=0)
     grad_ln2_bias = jnp.sum(normed2_grad, axis=0)
     stream_grad = cotangent + norm_backward(
@@ -186,9 +188,9 @@
     )
     stream_grad_b = stream_grad.astype(jnp.bfloat16)
     grad_out_bias = jnp.sum(stream_grad, axis=0)
-    grad_w_out = jnp.dot(attended.T, stream_grad_b, preferred_element_type=jnp.float32)
+    grad_w_out = over_rows(stream_grad_b, attended)
     attended_grad = (
-        jnp.dot(stream_grad_b, w_out.T, preferred_element_type=jnp.float32)
+        jnp.dot(stream_grad_b, w_out, preferred_element_type=jnp.float32)
         .astype(jnp.bfloat16)
         .reshape(head_shape)
     )
@@ -211,8 +213,8 @@
     grad_q_bias = jnp.sum(query_grad, axis=0)
     grad_v_bias = jnp.sum(value_grad, axis=0)
     qkv_grad = jnp.concatenate([query_grad, key_grad, value_grad], axis=1).astype(jnp.bfloat16)
-    grad_w_qkv = jnp.dot(normed1.T, qkv_grad, preferred_element_type=jnp.float32)
-    normed1_grad = jnp.dot(qkv_grad, w_qkv.T, preferred_element_type=jnp.float32)
+    grad_w_qkv = over_rows(normed1, qkv_grad)
+    normed1_grad = against(qkv_grad, w_qkv)
     grad_ln1_gain = jnp.sum(normed1_grad * scaled1, axis=0)
     grad_ln1_bias = jnp.sum(normed1_grad, axis=0)
     in_grad = (
@@ -238,42 +240,215 @@
     )
 
 
-def halving_sum(partial_value, shard_dims):
-    bit_total = lax.axis_size("fsdp").bit_length() - 1
-    own_index = lax.axis_index("fsdp")
-    for bit_number in range(bit_total - 1, -1, -1):
-        upper_bit = own_index >> bit_number & 1
-        kept_parts = []
-        sent_parts = []
-        for member, axis_dim in zip(partial_value, shard_dims):
-            half_len = member.shape[axis_dim] // 2
-            kept_parts.append(
-                lax.dynamic_slice_in_dim(member, upper_bit * half_len, half_len, axis_dim)
+def bit_orders(bit_total):
+    links = list(range(bit_total - 1, 0, -1))
+    if len(links) < 3:
+        return [links + [0]] * 4
+    high, second, last = links[:-2], links[-2], links[-1]
+    return [
+        high + [second, last, 0],
+        high + [last, second, 0],
+        [second] + high + [last, 0],
+        [last] + high + [second, 0],
+    ]
+
+
+def flipped(position, mask, bit_total):
+    for bit in range(bit_total):
+        if mask >> bit & 1:
+            position = position + (1 << bit) * (1 - 2 * (position // (1 << bit) % 2))
+    return position
+
+
+def greet(me, bit_total):
+    barrier = pltpu.get_barrier_semaphore()
+    for bit in range(bit_total):
+        pl.semaphore_signal(
+            barrier,
+            inc=1,
+            device_id=(flipped(me, 1 << bit, bit_total),),
+            device_id_type=pl.DeviceIdType.MESH,
+        )
+    pl.semaphore_wait(barrier, bit_total)
+
+
+def gather_kernel(bit_total, count, *refs):
+    shards, wholes = refs[:count], refs[count : 2 * count]
+    own_sem, send_sem, recv_sem = refs[2 * count :]
+    me = lax.axis_index("fsdp")
+    orders = bit_orders(bit_total)
+    greet(me, bit_total)
+    copies = []
+
+    def forward_shard(number, relative, first_step):
+        order = orders[number]
+        absolute = flipped(me, relative, bit_total)
+        for step in range(first_step, bit_total):
+            bit = order[step]
+            landed = relative ^ 1 << bit
+            source = shards[number] if relative == 0 else wholes[number].at[absolute]
+            copy = pltpu.make_async_remote_copy(
+                src_ref=source,
+                dst_ref=wholes[number].at[absolute],
+                send_sem=send_sem.at[number, landed],
+                recv_sem=recv_sem.at[number, landed],
+                device_id=(flipped(me, 1 << bit, bit_total),),
+                device_id_type=pl.DeviceIdType.MESH,
             )
-            sent_parts.append(
-                lax.dynamic_slice_in_dim(member, (1 - upper_bit) * half_len, half_len, axis_dim)
+            copy.start()
+            copies.append(copy)
+
+    for number in range(count):
+        forward_shard(number, 0, 0)
+    for number in range(count):
+        pltpu.make_async_copy(shards[number], wholes[number].at[me], own_sem.at[number]).start()
+    for turn in range(1, 1 << bit_total):
+        for number in range(count):
+            order = orders[number]
+            relative = sum(1 << order[step] for step in range(bit_total) if turn >> step & 1)
+            absolute = flipped(me, relative, bit_total)
+            arrival = pltpu.make_async_remote_copy(
+                src_ref=wholes[number].at[absolute],
+                dst_ref=wholes[number].at[absolute],
+                send_sem=send_sem.at[number, relative],
+                recv_sem=recv_sem.at[number, relative],
+                device_id=(flipped(me, 1, bit_total),),
+                device_id_type=pl.DeviceIdType.MESH,
             )
-        arrived = swapped(
-            (
-                as_sent(sent_parts[0]),
-                as_sent(sent_parts[1]),
-                as_sent(sent_parts[2]),
-                as_sent(sent_parts[3]),
-                as_sent(sent_parts[4]),
-                as_sent(sent_parts[5]),
-                as_sent(sent_parts[6]),
-                as_sent(sent_parts[7]),
-                as_sent(sent_parts[8]),
-                as_sent(sent_parts[9]),
-                as_sent(sent_parts[10]),
-                as_sent(sent_parts[11]),
-                as_sent(sent_parts[12]),
-            ),
-            "fsdp",
-            bit_number,
-        )
-        partial_value = tuple((kept + incoming for kept, incoming in zip(kept_parts, arrived)))
-    return partial_value
+            arrival.wait_recv()
+            forward_shard(number, relative, turn.bit_length())
+    for number in range(count):
+        pltpu.make_async_copy(shards[number], wholes[number].at[me], own_sem.at[number]).wait()
+    for copy in copies:
+        copy.wait_send()
+
+
+def gather_all(shards, parts):
+    count, bit_total = len(shards), parts.bit_length() - 1
+    return pl.pallas_call(
+        functools.partial(gather_kernel, bit_total, count),
+        out_shape=[jax.ShapeDtypeStruct((parts,) + s.shape, s.dtype) for s in shards],
+        in_specs=[pl.BlockSpec(memory_space=pltpu.VMEM)] * count,
+        out_specs=[pl.BlockSpec(memory_space=pl.ANY)] * count,
+        scratch_shapes=[
+            pltpu.SemaphoreType.DMA((count,)),
+            pltpu.SemaphoreType.DMA((count, parts)),
+            pltpu.SemaphoreType.DMA((count, parts)),
+        ],
+        compiler_params=pltpu.CompilerParams(collective_id=0, has_side_effects=True),
+    )(*shards)
+
+
+def first_step(relative, order):
+    for step, bit in enumerate(order):
+        if relative >> bit & 1:
+            return step
+    return len(order)
+
+
+def column_block(width):
+    for size in (768, 896, 640, 512, 384, 256, 128):
+        if width % size == 0:
+            return size
+    return width
+
+
+def scatter_kernel(bit_total, count, *refs):
+    terms, totals = refs[:count], refs[count : 2 * count]
+    landed = refs[2 * count : 3 * count]
+    send_sem, recv_sem = refs[3 * count :]
+    me = lax.axis_index("fsdp")
+    orders = [order[::-1] for order in bit_orders(bit_total)]
+    greet(me, bit_total)
+    copies = []
+
+
+    def place(number, relative, step):
+        bits = [bit for bit in orders[number][step + 1 :]]
+        index = sum(1 << i for i, bit in enumerate(bits) if relative >> bit & 1)
+        return sum(1 << bit_total - 1 - s for s in range(step)) + index
+
+    def summed(number, relative, steps, target):
+        absolute = flipped(me, relative, bit_total)
+        width = terms[number].shape[2]
+        size = column_block(width)
+        for step in range(steps):
+            slot = place(number, relative, step)
+            pltpu.make_async_remote_copy(
+                src_ref=landed[number].at[slot],
+                dst_ref=landed[number].at[slot],
+                send_sem=send_sem.at[number, slot],
+                recv_sem=recv_sem.at[number, slot],
+                device_id=(flipped(me, 1, bit_total),),
+                device_id_type=pl.DeviceIdType.MESH,
+            ).wait_recv()
+
+        def one(block, carry):
+            columns = pl.ds(pl.multiple_of(block * size, size), size)
+            total = terms[number][absolute, :, columns].astype(jnp.float32)
+            for step in range(steps):
+                total = total + landed[number][
+                    place(number, relative, step), :, columns
+                ].astype(jnp.float32)
+            target[:, columns] = total.astype(target.dtype)
+            return carry
+
+        lax.fori_loop(0, width // size, one, 0)
+
+    for step in range(bit_total):
+        names = []
+        for number in range(count):
+            order = orders[number]
+            later = [
+                sum(1 << order[step + 1 + i] for i in range(bit_total - 1 - step) if turn >> i & 1)
+                for turn in range(1 << bit_total - 1 - step)
+            ]
+            later.sort(key=lambda r: first_step(r, order))
+            names.append(later)
+        for turn in range(1 << bit_total - 1 - step):
+            for number in range(count):
+                order = orders[number]
+                kept = names[number][turn]
+                relative = kept | 1 << order[step]
+                absolute = flipped(me, relative, bit_total)
+                if step == 0:
+                    source = terms[number].at[absolute]
+                else:
+                    source = landed[number].at[place(number, relative, 0)]
+                    summed(number, relative, step, source)
+                slot = place(number, kept, step)
+                copy = pltpu.make_async_remote_copy(
+                    src_ref=source,
+                    dst_ref=landed[number].at[slot],
+                    send_sem=send_sem.at[number, slot],
+                    recv_sem=recv_sem.at[number, slot],
+                    device_id=(flipped(me, 1 << order[step], bit_total),),
+                    device_id_type=pl.DeviceIdType.MESH,
+                )
+                copy.start()
+                copies.append(copy)
+    for number in range(count):
+        summed(number, 0, bit_total, totals[number])
+    for copy in copies:
+        copy.wait_send()
+
+
+def scatter_all(terms, parts):
+    count, bit_total = len(terms), parts.bit_length() - 1
+    return pl.pallas_call(
+        functools.partial(scatter_kernel, bit_total, count),
+        out_shape=[jax.ShapeDtypeStruct(t.shape[1:], jnp.float32) for t in terms],
+        in_specs=[pl.BlockSpec(memory_space=pltpu.VMEM)] * count,
+        out_specs=[pl.BlockSpec(memory_space=pltpu.VMEM)] * count,
+        scratch_shapes=[pltpu.VMEM((parts - 1,) + t.shape[1:], t.dtype) for t in terms]
+        + [
+            pltpu.SemaphoreType.DMA((count, parts)),
+            pltpu.SemaphoreType.DMA((count, parts)),
+        ],
+        compiler_params=pltpu.CompilerParams(
+            collective_id=1, has_side_effects=True, vmem_limit_bytes=60 * 1024 * 1024
+        ),
+    )(*terms)
 
 
 def body(
@@ -294,47 +469,92 @@
     w_down,
     down_bias,
 ):
+    parts = lax.axis_size("fsdp")
     held_count = image_counts[0]
-    slot_count = block_in.shape[0]
-    shard_dims = (0, 0, 0, 0, 0, 1, 0, 0, 0, 0, 0, 1, 0)
+    slot_count, _, model_width = block_in.shape
+    rows = w_qkv.shape[0]
+    with_kernels = rows % 8 == 0 and parts & parts - 1 == 0
+    vectors = (ln1_gain, ln1_bias, q_bias, v_bias, out_bias, ln2_gain, ln2_bias, down_bias)
+    small = jnp.concatenate(
+        [jnp.stack(vectors, axis=1), up_bias.reshape(rows, -1)], axis=1
+    )
+    small_width = small.shape[1]
+    padding = -small_width % 128
+    small = jnp.pad(small, ((0, 0), (0, padding)))
+    shards = (w_qkv, jnp.concatenate([w_out.T, small], axis=1), w_up, w_down.T)
+    if with_kernels:
+        wholes = gather_all(shards, parts)
+    else:
+        wholes = [lax.all_gather(s, "fsdp", axis=0, tiled=False) for s in shards]
+    w_qkv, mixed, w_up, w_down = [w.reshape(parts * rows, w.shape[2]) for w in wholes]
+    w_out = mixed[:, :model_width]
+    small = mixed[:, model_width : model_width + small_width]
+    ln1_gain, ln1_bias, q_bias, v_bias, out_bias, ln2_gain, ln2_bias, down_bias = small[:, :8].T
+    up_bias = small[:, 8:].reshape(-1)
     gathered = (
-        lax.all_gather(ln1_gain, "fsdp", axis=0, tiled=True),
-        lax.all_gather(ln1_bias, "fsdp", axis=0, tiled=True),
-        lax.all_gather(w_qkv, "fsdp", axis=0, tiled=True),
-        lax.all_gather(q_bias, "fsdp", axis=0, tiled=True),
-        lax.all_gather(v_bias, "fsdp", axis=0, tiled=True),
-        lax.all_gather(w_out, "fsdp", axis=1, tiled=True),
-        lax.all_gather(out_bias, "fsdp", axis=0, tiled=True),
-        lax.all_gather(ln2_gain, "fsdp", axis=0, tiled=True),
-        lax.all_gather(ln2_bias, "fsdp", axis=0, tiled=True),
-        lax.all_gather(w_up, "fsdp", axis=0, tiled=True),
-        lax.all_gather(up_bias, "fsdp", axis=0, tiled=True),
-        lax.all_gather(w_down, "fsdp", axis=1, tiled=True),
-        lax.all_gather(down_bias, "fsdp", axis=0, tiled=True),
+        ln1_gain,
+        ln1_bias,
+        w_qkv,
+        q_bias,
+        v_bias,
+        w_out,
+        out_bias,
+        ln2_gain,
+        ln2_bias,
+        w_up,
+        up_bias,
+        w_down,
+        down_bias,
     )
     live_slots = (jnp.arange(slot_count, dtype=jnp.int32) < held_count)[:, None, None]
     result, stashed = forward(block_in, gathered)
     masked_grad = jnp.where(live_slots, out_grad, jnp.zeros_like(out_grad))
-    for_back = (
-        lax.all_gather(ln1_gain, "fsdp", axis=0, tiled=True),
-        lax.all_gather(ln1_bias, "fsdp", axis=0, tiled=True),
-        lax.all_gather(w_qkv, "fsdp", axis=0, tiled=True),
-        lax.all_gather(q_bias, "fsdp", axis=0, tiled=True),
-        lax.all_gather(v_bias, "fsdp", axis=0, tiled=True),
-        lax.all_gather(w_out, "fsdp", axis=1, tiled=True),
-        lax.all_gather(out_bias, "fsdp", axis=0, tiled=True),
-        lax.all_gather(ln2_gain, "fsdp", axis=0, tiled=True),
-        lax.all_gather(ln2_bias, "fsdp", axis=0, tiled=True),
-        lax.all_gather(w_up, "fsdp", axis=0, tiled=True),
-        lax.all_gather(up_bias, "fsdp", axis=0, tiled=True),
-        lax.all_gather(w_down, "fsdp", axis=1, tiled=True),
-        lax.all_gather(down_bias, "fsdp", axis=0, tiled=True),
-    )
-    back_rows, grad_terms = backward(masked_grad, for_back, stashed)
-    totals = halving_sum(grad_terms, shard_dims)
+    back_rows, grad_terms = backward(masked_grad, gathered, stashed)
     block_out = jnp.where(live_slots, result, jnp.zeros_like(result))
     in_grad = jnp.where(live_slots, back_rows, jnp.zeros_like(back_rows))
-    return (block_out, in_grad) + tuple(totals)
+
+    g_vectors = [grad_terms[i] for i in (0, 1, 3, 4, 6, 7, 8, 12)]
+    g_small = jnp.concatenate(
+        [jnp.stack(g_vectors, axis=1), grad_terms[10].reshape(parts * rows, -1)], axis=1
+    ).astype(jnp.bfloat16)
+    g_small = jnp.pad(g_small, ((0, 0), (0, padding)))
+    terms = (
+        grad_terms[2],
+        jnp.concatenate([grad_terms[5], g_small], axis=1),
+        grad_terms[9],
+        grad_terms[11],
+    )
+    terms = [t.reshape(parts, rows, t.shape[1]) for t in terms]
+    if with_kernels:
+        totals = scatter_all(terms, parts)
+    else:
+        totals = [
+            lax.psum_scatter(t.astype(jnp.float32), "fsdp", scatter_dimension=0, tiled=False)
+            for t in terms
+        ]
+    t_qkv, t_mixed, t_up, t_down = totals
+    t_out = t_mixed[:, :model_width].T
+    t_small = t_mixed[:, model_width : model_width + small_width]
+    t_ln1_gain, t_ln1_bias, t_q, t_v, t_out_bias, t_ln2_gain, t_ln2_bias, t_down_bias = t_small[
+        :, :8
+    ].T
+    return (
+        block_out,
+        in_grad,
+        t_ln1_gain,
+        t_ln1_bias,
+        t_qkv,
+        t_q,
+        t_v,
+        t_out,
+        t_out_bias,
+        t_ln2_gain,
+        t_ln2_bias,
+        t_up,
+        t_small[:, 8:].reshape(-1),
+        t_down.T,
+        t_down_bias,
+    )
 
 
 def solution(mesh):

time: 781 us -> 272 us (0.35)
  waiting for transfers between devices: 516 us -> 0 us
  Pallas kernels: 0 us -> 162 us
  starting transfers between devices: 77.4 us -> 0 us
  blocking collectives: 41.2 us -> 0 us
  between operations: 15.7 us -> 2.06 us
  other arithmetic: 23.5 us -> 10.3 us
    ppermute x65 -> x0, waiting for transfers between devices: 352 us -> none  [swapped(): lax.ppermute(value, axis, [(i, i ^ 1 << stride) for i in range(lax.axis_s...]
    pallas_call x0 -> x2, Pallas kernels: none -> 162 us  [the longest x1 93.7 us: scatter_all(): pl.pallas_call(functools.partial(scatter_kernel, bit_total, count), out_s...]
    all_gather x4 -> x0, waiting for transfers between devices: 161 us -> none  [the longest x1 63.3 us: body(): lax.all_gather(w_up, 'fsdp', axis=0, tiled=True)]
    ppermute x65 -> x0, starting transfers between devices: 77.3 us -> none  [swapped(): lax.ppermute(value, axis, [(i, i ^ 1 << stride) for i in range(lax.axis_s...]
    unnamed x1 -> x0, blocking collectives: 41.2 us -> none
    add x65 -> x1, other arithmetic: 17.3 us -> 0.09 us  [forward(): stream + against(activated, w_down) + down_bias.astype(jnp.float32)]
    another operation x1 -> x18, local copies, waits for them, and re-layouts: 2.16 us -> 12.8 us  [the longest x8 5.98 us: body(): jnp.stack(vectors, axis=1)]
    convert_element_type x20 -> x3, local copies, waits for them, and re-layouts: 10.4 us -> 0.32 us  [the longest x1 0.22 us: forward(): up_bias.astype(jnp.float32)]
  transfers between devices with their start and end apart: 69 -> 0, of which waited for: 50 -> 0; matrix products, arithmetic and copies ran while one was open for 8% -> 0% of each run, Pallas kernels for 0% -> 0%
where the time goes in v1:
time: 272 us; the launch traced here: 270 us
  Pallas kernels  162 us (60%)
  local copies, waits for them, and re-layouts  51.9 us (19%)
  matrix products  44 us (16%)
  other arithmetic  10.3 us (4%)
    pallas_call x1, Pallas kernels, scatter_all(): pl.pallas_call(functools.partial(scatter_kernel, bit_total, count), out_s...  93.7 us
    pallas_call x1, Pallas kernels, gather_all(): pl.pallas_call(functools.partial(gather_kernel, bit_total, count), out_sh...  68.3 us
    dot_general x4, matrix products, over_rows(): lax.dot_general(left, right, (((0,), (0,)), ((), ())), preferred_element_...  12.2 us
    dot_general x4, matrix products, against(): lax.dot_general(left, right, (((1,), (1,)), ((), ())), preferred_element_...  10.9 us
    unnamed x80, local copies, waits for them, and re-layouts  9.83 us
    dot_general x6, matrix products, mixing(): return jnp.einsum(form, left, right, preferred_element_type=jnp.float32)  7.58 us
    another operation x8, local copies, waits for them, and re-layouts, body(): jnp.stack(vectors, axis=1)  5.98 us
    dot_general x1, matrix products, backward(): jnp.dot(grad_rows, w_down, preferred_element_type=jnp.float32)  5.59 us

profile of v1, /device:TPU:0, one launch (start us, length us, event | category | flops | bytes accessed | tf_op | source)
XLA Modules:
  0.0 270.3 jit_solution(8499831976638094656)
XLA Ops:
  1.4 0.7 copy.137
  2.1 0.7 copy.138
  2.9 0.7 copy.139
  3.6 0.7 copy.140
  4.4 0.7 copy.141
  5.1 0.7 copy.142
  5.9 0.7 copy.143
  6.6 0.7 reshape.216
  7.4 0.8 copy.144
  8.2 1.4 fusion.29.refs_1_
  9.6 1.3 convert_reduce_fusion
  11.1 1.6 multiply_reduce_fusion.6
  12.8 0.7 rsqrt.22
  13.6 0.6 stack.71
  14.4 68.3 %shard_map.271 = (bf16[32,24,2304]{2,1,0:T(8,128)(2,1)}, bf16[32,24,896]{2,1,0:T(8,128)(2,1)}, bf16[32,24,3072]{2,1,0:T(8,128)(2,1)}, bf16[32,24,3072]{2,1,0:T(8,128)(2,1)}) custom-call(bf16[24,2304]{1,0:T(8,128)(2,1)} %refs_0_.1, bf16[24,896]{1,0:T(8,128)(2,1)} %fusion.29.refs_1_, bf16[24,3072]{1,0:T(8,128)(2,1)} %refs_2_.1, bf16[24,3072]{1,0:T(8,128)(2,1)} %bitcast.80), custom_call_target="tpu_custom_call" | custom-call | tf_op jit(solution)/shard_map/pallas_call | solution.py:328
  82.8 0.9 slice.43
  84.6 1.0 slice_convert_fusion.1
  85.9 2.9 %fusion.45 = f32[202,2304]{1,0:T(8,128)S(1)} fusion(bf16[202,768]{1,0:T(8,128)(2,1)S(1)} %convert_element_type.119, bf16[768,2304]{1,0:T(8,128)(2,1)} %bitcast.77), kind=kOutput, calls=%fused_computation.121 | convolution fusion | flops 714866688 | bytes 5710848 | tf_op jit(solution)/shard_map/dot_general | solution.py:87
  89.4 0.6 copy.150
  90.6 1.4 copy.151
  92.4 0.6 copy.152
  93.1 1.7 fusion.42
  96.1 2.1 fusion.43
  98.4 3.6 %multiply_convert_fusion = (bf16[202,3072]{1,0:T(8,128)(2,1)S(1)}, f32[202,3072]{1,0:T(8,128)S(1)}) fusion(f32[3072]{0:T(1024)S(1)} %reshape.244, bf16[768,3072]{1,0:T(8,128)(2,1)} %bitcast.91, f32[202,768]{1,0:T(8,128)S(1)} %get-tuple-element.115, f32[768]{0:T(1024)S(1)} %get-tuple-element.93, f32[768]{0:T(1024)S(1)} %get-tuple-element.94, ...), kind=kOutput, calls=%fused_computation.12 | convolution fusion | flops 957654528 | bytes 9082448 | tf_op jit(solution)/shard_map/dot_general | solution.py:110
  102.1 5.6 %fusion.44 = (bf16[3072]{0:T(1024)(128)(2,1)}, bf16[202,3072]{1,0:T(8,128)(2,1)S(1)}) fusion(f32[202,3072]{1,0:T(8,128)S(1)} %get-tuple-element.122, bf16[202,768]{1,0:T(8,128)(2,1)S(1)} %reshape.225, bf16[768,3072]{1,0:T(8,128)(2,1)} %bitcast.95), kind=kOutput, calls=%fused_computation.120 | convolution fusion | flops 959978496 | bytes 8758272 | tf_op jit(solution)/shard_map/dot_general | solution.py:177
  107.7 1.7 fusion.8
  109.4 3.2 %multiply_reduce_fusion.1 = (bf16[768]{0:T(1024)(128)(2,1)S(1)}, f32[202]{0:T(256)S(1)}, f32[202]{0:T(256)S(1)}, bf16[768]{0:T(1024)(128)(2,1)}, f32[202,768]{1,0:T(8,128)}) fusion(f32[202,768]{1,0:T(8,128)S(1)} %get-tuple-element.115, f32[202]{0:T(256)S(1)} %add_rsqrt_fusion.1, f32[202]{0:T(256)S(1)} %broadcast_multiply_fusion.5, ...), kind=kOutput, calls=%fused_computation.41 | convolution fusion | flops 954549888 | bytes 7210144 | tf_op jit(solution)/shard_map/dot_general | solution.py:24
  112.6 0.8 reshape.224
  114.0 1.4 fusion.39
  115.4 1.1 convolution_convert_fusion.6
  117.7 1.8 reshape.231
  119.5 1.6 copy.168
  121.1 2.4 reshape.249
  123.6 2.4 copy.157
  126.0 2.9 %fusion.40 = (bf16[12,64]{1,0:T(8,128)(2,1)}, bf16[2,101,12,64]{1,3,2,0:T(8,128)(2,1)}) fusion(bf16[2,101,12,64]{1,3,2,0:T(8,128)(2,1)} %copy.157, f32[2,12,101,101]{2,3,1,0:T(8,128)S(1)} %get-tuple-element.113, f32[2,12,101]{2,1,0:T(8,128)S(1)} %log_add_fusion), kind=kOutput, calls=%fused_computation.116 | convolution fusion | flops 32136624 | bytes 1611072 | tf_op jit(solution)/shard_map/bhqk,bqhd->bkhd/dot_general | solution.py:20
  128.9 1.3 stack.67
  130.3 2.2 copy.167
  132.4 2.0 reshape.228
  134.5 1.7 multiply_reduce_fusion
  136.5 0.7 copy-done.4
  139.1 1.0 reshape.227
  140.5 1.0 mul.200
  141.4 1.1 constant_dynamic-update-slice_fusion.2
  142.5 1.0 constant_dynamic-update-slice_fusion.1
  143.6 4.0 %multiply_reduce_fusion.2 = (bf16[768]{0:T(1024)(128)(2,1)S(1)}, f32[202]{0:T(256)S(1)}, f32[202]{0:T(256)S(1)}, bf16[768]{0:T(1024)(128)(2,1)S(1)}, f32[202,768]{1,0:T(8,128)S(1)}) fusion(f32[202,768]{1,0:T(8,128)S(1)} %reshape.236, f32[202]{0:T(256)S(1)} %div.33, f32[202]{0:T(256)S(1)} %copy-done.20, f32[768]{0:T(1024)S(1)} %get-tuple-element.99, ...), kind=kOutput, calls=%fused_computation.42 | convolution fusion | flops 716260992 | bytes 5720224 | tf_op jit(solution)/shard_map/dot_general | solution.py:24
  147.6 1.0 add_convert_fusion.1
  148.6 1.1 reshape.229
  149.8 0.8 broadcast_select_fusion
  150.6 1.0 copy.171
  151.6 1.3 concatenate.20
  153.7 1.6 copy.169
  155.3 1.0 copy.170
  156.2 4.5 %convolution_convert_fusion = bf16[768,2304]{1,0:T(8,128)(2,1)} fusion(bf16[202,2304]{0,1:T(8,128)(2,1)} %copy-done.8, f32[202,768]{1,0:T(8,128)S(1)} %reshape.236, f32[768]{0:T(1024)S(1)} %get-tuple-element.98, f32[202]{0:T(256)S(1)} %div.33, f32[768]{0:T(1024)S(1)} %get-tuple-element.99, f32[202]{0:T(256)S(1)} %copy-done.20), kind=kOutput, calls=%fused_computation | convolution fusion | flops 717411840 | bytes 5098064 | tf_op jit(solution)/shard_map/dot_general | solution.py:28
  160.7 3.7 %convolution_convert_fusion.2 = bf16[768,3072]{1,0:T(8,128)(2,1)} fusion(bf16[202,3072]{1,0:T(8,128)(2,1)S(1)} %copy-done.15, f32[202,768]{1,0:T(8,128)S(1)} %get-tuple-element.115, f32[768]{0:T(1024)S(1)} %get-tuple-element.93, f32[768]{0:T(1024)S(1)} %get-tuple-element.94, f32[202]{0:T(256)S(1)} %copy-done.22, f32[202]{0:T(256)S(1)} %broadcast_multiply_fusion.5), kind=kOutput, calls=%fused_computation.2 | convolution fusion | flops 956290560 | bytes 6587984 | tf_op jit(solution)/shard_map/dot_general | solution.py:28
  164.4 3.6 %convolution_convert_fusion.1 = bf16[768,3072]{1,0:T(8,128)(2,1)} fusion(bf16[202,768]{1,0:T(8,128)(2,1)S(1)} %reshape.225, bf16[202,3072]{1,0:T(8,128)(2,1)S(1)} %copy-done.13), kind=kOutput, calls=%fused_computation.1 | convolution fusion | flops 955514880 | bytes 6269952 | tf_op jit(solution)/shard_map/dot_general | solution.py:28
  168.0 93.7 %shard_map.272 = (f32[24,2304]{1,0:T(8,128)}, f32[24,896]{1,0:T(8,128)}, f32[24,3072]{1,0:T(8,128)}, f32[24,3072]{1,0:T(8,128)}) custom-call(bf16[32,24,2304]{2,1,0:T(8,128)(2,1)} %bitcast.71, bf16[32,24,896]{2,1,0:T(8,128)(2,1)} %bitcast.72, bf16[32,24,3072]{2,1,0:T(8,128)(2,1)} %bitcast.69, bf16[32,24,3072]{2,1,0:T(8,128)(2,1)} %bitcast.70), custom_call_target="tpu_custom_call" | custom-call | tf_op jit(solution)/shard_map/pallas_call | solution.py:438
  261.8 0.8 slice.42
  262.6 0.6 reshape.235
  263.2 0.7 slice_bitcast_fusion.1
  263.9 1.5 slice_bitcast_fusion
  265.4 0.8 slice_reduce_fusion
  266.2 1.6 copy.195
  267.9 1.7 copy.196
  269.6 0.7 copy.197
  (119 shorter events, 10.2 us)
Async XLA Ops:
  0.6 13.6 %copy-start.1 = (bf16[2,101,768]{2,0,1:T(2,128)(2,1)S(1)}, bf16[2,101,768]{2,0,1:T(2,128)(2,1)}, u32[]{:S(2)}) copy-start(bf16[2,101,768]{2,0,1:T(2,128)(2,1)} %param.16) | copy-start | bytes 930820
  0.7 12.8 %copy-start.16 = (bf16[2,101,768]{2,0,1:T(2,128)(2,1)S(1)}, bf16[2,101,768]{2,0,1:T(2,128)(2,1)}, u32[]{:S(2)}) copy-start(bf16[2,101,768]{2,0,1:T(2,128)(2,1)} %param.17) | copy-start | bytes 930820
  1.4 12.9 %copy-start.29 = (pred[2]{0:T(512)(128)(4,1)}, pred[2]{0:T(512)(128)(4,1)S(1)}, u32[]{:S(2)}) copy-start(pred[2]{0:T(512)(128)(4,1)S(1)} %iota_compare_fusion.2) | copy-start | bytes 10
  90.1 3.0 %copy-start.3 = (bf16[2,101,12,64]{1,3,2,0:T(8,128)(2,1)}, bf16[2,101,12,64]{1,3,2,0:T(8,128)(2,1)S(1)}, u32[]{:S(2)}) copy-start(bf16[2,101,12,64]{1,3,2,0:T(8,128)(2,1)S(1)} %copy.150) | copy-start | bytes 930820
  93.1 2.0 copy-start.2
  96.1 2.1 copy-start.6
  98.4 11.0 %copy-start.21 = (f32[202]{0:T(256)}, f32[202]{0:T(256)S(1)}, u32[]{:S(2)}) copy-start(f32[202]{0:T(256)S(1)} %add_rsqrt_fusion.1) | copy-start | bytes 2428
  98.4 9.3 %slice-start.2 = ((s8[4718592]{0:T(1024)(128)(4,1)}), s8[4194304]{0:T(1024)(128)(4,1)S(1)}, s32[]{:S(2)}) async-start(s8[4718592]{0:T(1024)(128)(4,1)} %bitcast.96), calls=%async_computation.2 | async-start | bytes 8388608
  98.4 11.0 %slice-start = ((s8[4718592]{0:T(1024)(128)(4,1)}), s8[4194304]{0:T(1024)(128)(4,1)S(1)}, s32[]{:S(2)}) async-start(s8[4718592]{0:T(1024)(128)(4,1)} %bitcast.92), calls=%async_computation | async-start | bytes 8388608
  102.1 5.6 %copy-start.12 = (bf16[202,3072]{1,0:T(8,128)(2,1)}, bf16[202,3072]{1,0:T(8,128)(2,1)S(1)}, u32[]{:S(2)}) copy-start(bf16[202,3072]{1,0:T(8,128)(2,1)S(1)} %get-tuple-element.121) | copy-start | bytes 3723268
  102.1 5.6 %slice-start.3 = ((s8[4718592]{0:T(1024)(128)(4,1)}), s8[524288]{0:T(1024)(128)(4,1)S(1)}, s32[]{:S(2)}) async-start(s8[4718592]{0:T(1024)(128)(4,1)} %bitcast.96), calls=%async_computation.3 | async-start | bytes 1048576
  102.1 7.3 %slice-start.1 = ((s8[4718592]{0:T(1024)(128)(4,1)}), s8[524288]{0:T(1024)(128)(4,1)S(1)}, s32[]{:S(2)}) async-start(s8[4718592]{0:T(1024)(128)(4,1)} %bitcast.92), calls=%async_computation.1 | async-start | bytes 1048576
  107.7 1.7 copy-start.14
  113.4 2.0 copy-start
  115.4 1.8 copy-start.28
  136.2 1.0 copy-start.4
  137.1 1.0 copy-start.5
  141.4 2.1 copy-start.9
  141.4 2.2 copy-start.20
  143.6 4.0 %copy-start.8 = (bf16[202,2304]{0,1:T(8,128)(2,1)}, bf16[202,2304]{0,1:T(8,128)(2,1)S(1)}, u32[]{:S(2)}) copy-start(bf16[202,2304]{0,1:T(8,128)(2,1)S(1)} %constant_dynamic-update-slice_fusion) | copy-start | bytes 2792452
  147.6 2.1 copy-start.10
  147.6 2.1 copy-start.30
  148.6 2.9 %copy-start.19 = (bf16[768,4]{0,1:T(4,128)(2,1)S(1)}, bf16[768,4]{0,1:T(4,128)(2,1)}, u32[]{:S(2)}) copy-start(bf16[768,4]{0,1:T(4,128)(2,1)} %copy.168) | copy-start | bytes 18436
  148.6 2.9 %copy-start.23 = (bf16[768,1]{0,1:T(2,128)(2,1)S(1)}, bf16[768,1]{0,1:T(2,128)(2,1)}, u32[]{:S(2)}) copy-start(bf16[768,1]{0,1:T(2,128)(2,1)} %stack.67) | copy-start | bytes 4612
  148.6 2.9 %copy-start.24 = (bf16[768,1]{0,1:T(2,128)(2,1)S(1)}, bf16[768,1]{0,1:T(2,128)(2,1)}, u32[]{:S(2)}) copy-start(bf16[768,1]{0,1:T(2,128)(2,1)} %stack.71) | copy-start | bytes 4612
  148.6 3.0 %copy-start.25 = (bf16[768,1]{0,1:T(2,128)(2,1)S(1)}, bf16[768,1]{0,1:T(2,128)(2,1)}, u32[]{:S(2)}) copy-start(bf16[768,1]{0,1:T(2,128)(2,1)} %stack.69) | copy-start | bytes 4612
  148.6 3.0 %copy-start.26 = (bf16[768,1]{0,1:T(2,128)(2,1)S(1)}, bf16[768,1]{0,1:T(2,128)(2,1)}, u32[]{:S(2)}) copy-start(bf16[768,1]{0,1:T(2,128)(2,1)} %stack.68) | copy-start | bytes 4612
  148.6 3.0 %copy-start.27 = (bf16[768,1]{0,1:T(2,128)(2,1)S(1)}, bf16[768,1]{0,1:T(2,128)(2,1)}, u32[]{:S(2)}) copy-start(bf16[768,1]{0,1:T(2,128)(2,1)} %stack.70) | copy-start | bytes 4612
  148.6 4.2 %copy-start.7 = (bf16[202,768]{0,1:T(8,128)(2,1)S(1)}, bf16[202,768]{0,1:T(8,128)(2,1)}, u32[]{:S(2)}) copy-start(bf16[202,768]{0,1:T(8,128)(2,1)} %copy-done.6) | copy-start | bytes 930820
  152.9 0.7 copy-start.18
  153.7 1.6 copy-start.11
  156.2 4.5 %copy-start.15 = (bf16[202,3072]{1,0:T(8,128)(2,1)S(1)}, bf16[202,3072]{1,0:T(8,128)(2,1)}, u32[]{:S(2)}) copy-start(bf16[202,3072]{1,0:T(8,128)(2,1)} %copy-done.14) | copy-start | bytes 3723268
  156.2 4.5 %copy-start.22 = (f32[202]{0:T(256)S(1)}, f32[202]{0:T(256)}, u32[]{:S(2)}) copy-start(f32[202]{0:T(256)} %copy-done.21) | copy-start | bytes 2428
  160.7 3.7 %copy-start.13 = (bf16[202,3072]{1,0:T(8,128)(2,1)S(1)}, bf16[202,3072]{1,0:T(8,128)(2,1)}, u32[]{:S(2)}) copy-start(bf16[202,3072]{1,0:T(8,128)(2,1)} %copy-done.12) | copy-start | bytes 3723268
  261.7 7.8 %copy-start.17 = (f32[24,3072]{1,0:T(8,128)S(1)}, f32[24,3072]{1,0:T(8,128)}, u32[]{:S(2)}) copy-start(f32[24,3072]{1,0:T(8,128)} %get-tuple-element.30) | copy-start | bytes 884740

commit v2 on v1

--- a/solution.py
+++ b/solution.py
@@ -355,22 +355,30 @@
 
 def scatter_kernel(bit_total, count, *refs):
     terms, totals = refs[:count], refs[count : 2 * count]
-    landed = refs[2 * count : 3 * count]
-    send_sem, recv_sem = refs[3 * count :]
+    landed, held = refs[2 * count : 3 * count], refs[3 * count : 4 * count]
+    send_sem, recv_sem, load_sem = refs[4 * count :]
     me = lax.axis_index("fsdp")
     orders = [order[::-1] for order in bit_orders(bit_total)]
     greet(me, bit_total)
     copies = []
 
 
+    def load(number, relative):
+        absolute = flipped(me, relative, bit_total)
+        return pltpu.make_async_copy(
+            terms[number].at[absolute],
+            held[number].at[relative // 2],
+            load_sem.at[number, relative // 2],
+        )
+
     def place(number, relative, step):
         bits = [bit for bit in orders[number][step + 1 :]]
         index = sum(1 << i for i, bit in enumerate(bits) if relative >> bit & 1)
         return sum(1 << bit_total - 1 - s for s in range(step)) + index
 
     def summed(number, relative, steps, target):
-        absolute = flipped(me, relative, bit_total)
         width = terms[number].shape[2]
+        load(number, relative).wait()
         size = column_block(width)
         for step in range(steps):
             slot = place(number, relative, step)
@@ -385,7 +393,7 @@
 
         def one(block, carry):
             columns = pl.ds(pl.multiple_of(block * size, size), size)
-            total = terms[number][absolute, :, columns].astype(jnp.float32)
+            total = held[number][relative // 2, :, columns].astype(jnp.float32)
             for step in range(steps):
                 total = total + landed[number][
                     place(number, relative, step), :, columns
@@ -427,6 +435,10 @@
                 )
                 copy.start()
                 copies.append(copy)
+        if step == 0:
+            for turn in range(1 << bit_total - 1):
+                for number in range(count):
+                    load(number, names[number][turn]).start()
     for number in range(count):
         summed(number, 0, bit_total, totals[number])
     for copy in copies:
@@ -438,10 +450,12 @@
     return pl.pallas_call(
         functools.partial(scatter_kernel, bit_total, count),
         out_shape=[jax.ShapeDtypeStruct(t.shape[1:], jnp.float32) for t in terms],
-        in_specs=[pl.BlockSpec(memory_space=pltpu.VMEM)] * count,
+        in_specs=[pl.BlockSpec(memory_space=pl.ANY)] * count,
         out_specs=[pl.BlockSpec(memory_space=pltpu.VMEM)] * count,
         scratch_shapes=[pltpu.VMEM((parts - 1,) + t.shape[1:], t.dtype) for t in terms]
+        + [pltpu.VMEM((parts // 2,) + t.shape[1:], t.dtype) for t in terms]
         + [
+            pltpu.SemaphoreType.DMA((count, parts)),
             pltpu.SemaphoreType.DMA((count, parts)),
             pltpu.SemaphoreType.DMA((count, parts)),
         ],
@@ -475,9 +489,7 @@
     rows = w_qkv.shape[0]
     with_kernels = rows % 8 == 0 and parts & parts - 1 == 0
     vectors = (ln1_gain, ln1_bias, q_bias, v_bias, out_bias, ln2_gain, ln2_bias, down_bias)
-    small = jnp.concatenate(
-        [jnp.stack(vectors, axis=1), up_bias.reshape(rows, -1)], axis=1
-    )
+    small = jnp.concatenate(vectors + (up_bias,)).reshape(rows, -1)
     small_width = small.shape[1]
     padding = -small_width % 128
     small = jnp.pad(small, ((0, 0), (0, padding)))
@@ -488,9 +500,11 @@
         wholes = [lax.all_gather(s, "fsdp", axis=0, tiled=False) for s in shards]
     w_qkv, mixed, w_up, w_down = [w.reshape(parts * rows, w.shape[2]) for w in wholes]
     w_out = mixed[:, :model_width]
-    small = mixed[:, model_width : model_width + small_width]
-    ln1_gain, ln1_bias, q_bias, v_bias, out_bias, ln2_gain, ln2_bias, down_bias = small[:, :8].T
-    up_bias = small[:, 8:].reshape(-1)
+    small = mixed[:, model_width : model_width + small_width].reshape(parts, -1)
+    ln1_gain, ln1_bias, q_bias, v_bias, out_bias, ln2_gain, ln2_bias, down_bias = [
+        small[:, i * rows : (i + 1) * rows].reshape(-1) for i in range(8)
+    ]
+    up_bias = small[:, 8 * rows :].reshape(-1)
     gathered = (
         ln1_gain,
         ln1_bias,
@@ -515,8 +529,8 @@
 
     g_vectors = [grad_terms[i] for i in (0, 1, 3, 4, 6, 7, 8, 12)]
     g_small = jnp.concatenate(
-        [jnp.stack(g_vectors, axis=1), grad_terms[10].reshape(parts * rows, -1)], axis=1
-    ).astype(jnp.bfloat16)
+        [g.astype(jnp.bfloat16).reshape(parts, -1) for g in g_vectors + [grad_terms[10]]], axis=1
+    ).reshape(parts * rows, -1)
     g_small = jnp.pad(g_small, ((0, 0), (0, padding)))
     terms = (
         grad_terms[2],
@@ -534,10 +548,10 @@
         ]
     t_qkv, t_mixed, t_up, t_down = totals
     t_out = t_mixed[:, :model_width].T
-    t_small = t_mixed[:, model_width : model_width + small_width]
-    t_ln1_gain, t_ln1_bias, t_q, t_v, t_out_bias, t_ln2_gain, t_ln2_bias, t_down_bias = t_small[
-        :, :8
-    ].T
+    t_small = t_mixed[:, model_width : model_width + small_width].reshape(-1)
+    t_ln1_gain, t_ln1_bias, t_q, t_v, t_out_bias, t_ln2_gain, t_ln2_bias, t_down_bias = [
+        t_small[i * rows : (i + 1) * rows] for i in range(8)
+    ]
     return (
         block_out,
         in_grad,
@@ -551,7 +565,7 @@
         t_ln2_gain,
         t_ln2_bias,
         t_up,
-        t_small[:, 8:].reshape(-1),
+        t_small[8 * rows :],
         t_down.T,
         t_down_bias,
     )

time: 272 us -> 272 us (level)
  Pallas kernels: 162 us -> 158 us
    another operation x18 -> x1, local copies, waits for them, and re-layouts: 12.8 us -> 2.17 us  [the longest x8 5.98 us: body(): jnp.stack(vectors, axis=1)]
    convert_element_type x0 -> x16, local copies, waits for them, and re-layouts: none -> 7.1 us  [the longest x8 6.45 us: body(): g.astype(jnp.bfloat16).reshape(parts, -1)]
    slice x2 -> x12, local copies, waits for them, and re-layouts: 1.77 us -> 7.81 us  [the longest x9 5.55 us: body(): t_small[i * rows:(i + 1) * rows]]
    concatenate x2, local copies, waits for them, and re-layouts: 1.37 us -> 6.22 us  [the longest x1 6.11 us: body(): small = jnp.concatenate(vectors + (up_bias,)).reshape(rows, -1)]
    reshape x4 -> x5, local copies, waits for them, and re-layouts: 4.8 us -> 0.67 us  [the longest x2 0.32 us: body(): g_small = jnp.concatenate([g.astype(jnp.bfloat16).reshape(parts, -1) for...]
    pallas_call x1, Pallas kernels: 93.7 us -> 89.9 us  [scatter_all(): pl.pallas_call(functools.partial(scatter_kernel, bit_total, count), out_s...]
    unnamed x80 -> x83, local copies, waits for them, and re-layouts: 9.83 us -> 9.53 us
where the time goes in v2:
time: 272 us; the launch traced here: 271 us
  Pallas kernels  158 us (58%)
  local copies, waits for them, and re-layouts  54.6 us (20%)
  matrix products  44.4 us (16%)
  other arithmetic  11.3 us (4%)
    pallas_call x1, Pallas kernels, scatter_all(): pl.pallas_call(functools.partial(scatter_kernel, bit_total, count), out_s...  89.9 us
    pallas_call x1, Pallas kernels, gather_all(): pl.pallas_call(functools.partial(gather_kernel, bit_total, count), out_sh...  68.3 us
    dot_general x4, matrix products, over_rows(): lax.dot_general(left, right, (((0,), (0,)), ((), ())), preferred_element_...  13.2 us
    dot_general x4, matrix products, against(): lax.dot_general(left, right, (((1,), (1,)), ((), ())), preferred_element_...  10.8 us
    unnamed x83, local copies, waits for them, and re-layouts  9.53 us
    dot_general x6, matrix products, mixing(): return jnp.einsum(form, left, right, preferred_element_type=jnp.float32)  7.59 us
    convert_element_type x8, local copies, waits for them, and re-layouts, body(): g.astype(jnp.bfloat16).reshape(parts, -1)  6.45 us
    concatenate x1, local copies, waits for them, and re-layouts, body(): small = jnp.concatenate(vectors + (up_bias,)).reshape(rows, -1)  6.11 us

profile of v2, /device:TPU:0, one launch (start us, length us, event | category | flops | bytes accessed | tf_op | source)
XLA Modules:
  0.0 270.7 jit_solution(11918718378247096421)
XLA Ops:
  1.4 6.1 %concatenate.16 = bf16[288]{0:T(512)(128)(2,1)S(1)} concatenate(bf16[24]{0:T(256)(128)(2,1)} %param.19, bf16[24]{0:T(256)(128)(2,1)} %param.20, bf16[24]{0:T(256)(128)(2,1)} %param.22, bf16[24]{0:T(256)(128)(2,1)} %param.23, bf16[24]{0:T(256)(128)(2,1)} %param.25, bf16[24]{0:T(256)(128)(2,1)} %param.26, bf16[24]{0:T(256)(128)(2,1)} %param.27, bf16[24]{0:T(256)(128)(2,1)} %param.31, ...), dimensions={0} | concatenate | bytes 1152 | tf_op jit(solution)/shard_map/concatenate | solution.py:492
  7.6 1.4 fusion.29.refs_1_
  9.0 1.3 convert_reduce_fusion
  10.4 0.7 div.33
  11.1 1.6 multiply_reduce_fusion.6
  12.7 0.7 rsqrt.22
  13.9 68.3 %shard_map.271 = (bf16[32,24,2304]{2,1,0:T(8,128)(2,1)}, bf16[32,24,896]{2,1,0:T(8,128)(2,1)}, bf16[32,24,3072]{2,1,0:T(8,128)(2,1)}, bf16[32,24,3072]{2,1,0:T(8,128)(2,1)}) custom-call(bf16[24,2304]{1,0:T(8,128)(2,1)} %refs_0_.1, bf16[24,896]{1,0:T(8,128)(2,1)} %fusion.29.refs_1_, bf16[24,3072]{1,0:T(8,128)(2,1)} %refs_2_.1, bf16[24,3072]{1,0:T(8,128)(2,1)} %bitcast.68), custom_call_target="tpu_custom_call" | custom-call | tf_op jit(solution)/shard_map/pallas_call | solution.py:328
  82.2 0.9 slice.143
  84.9 2.9 %fusion.38 = f32[202,2304]{1,0:T(8,128)S(1)} fusion(bf16[202,768]{1,0:T(8,128)(2,1)S(1)} %convert_element_type.240, bf16[768,2304]{1,0:T(8,128)(2,1)} %bitcast.65), kind=kOutput, calls=%fused_computation.105 | convolution fusion | flops 714866688 | bytes 5710848 | tf_op jit(solution)/shard_map/dot_general | solution.py:87
  88.5 0.6 copy.115
  89.7 1.4 copy.116
  91.5 0.6 copy.117
  92.2 1.7 fusion.35
  95.2 2.1 fusion.36
  97.5 3.6 %multiply_convert_fusion = (bf16[202,3072]{1,0:T(8,128)(2,1)S(1)}, f32[202,3072]{1,0:T(8,128)S(1)}) fusion(f32[3072]{0:T(1024)S(1)} %reshape.343, bf16[768,3072]{1,0:T(8,128)(2,1)} %bitcast.70, f32[202,768]{1,0:T(8,128)S(1)} %get-tuple-element.115, f32[768]{0:T(1024)S(1)} %reshape.342, f32[768]{0:T(1024)S(1)} %reshape.341, f32[202]{0:T(256)S(1)} %add_rsqrt_fusion.1, ...), kind=kOutput, calls=%fused_computation.12 | convolution fusion | flops 957654528 | bytes 9082448 | tf_op jit(solution)/shard_map/dot_general | solution.py:110
  101.2 5.0 %fusion.37 = (bf16[3072]{0:T(1024)(128)(2,1)S(1)}, bf16[202,3072]{1,0:T(8,128)(2,1)S(1)}) fusion(f32[202,3072]{1,0:T(8,128)S(1)} %get-tuple-element.124, bf16[202,768]{1,0:T(8,128)(2,1)S(1)} %reshape.324, bf16[768,3072]{1,0:T(8,128)(2,1)} %bitcast.74), kind=kOutput, calls=%fused_computation.104 | convolution fusion | flops 959978496 | bytes 8758272 | tf_op jit(solution)/shard_map/dot_general | solution.py:177
  106.2 1.6 fusion.8
  107.9 3.2 %multiply_reduce_fusion.1 = (bf16[768]{0:T(1024)(128)(2,1)}, f32[202]{0:T(256)S(1)}, f32[202]{0:T(256)S(1)}, bf16[768]{0:T(1024)(128)(2,1)}, f32[202,768]{1,0:T(8,128)}) fusion(f32[202,768]{1,0:T(8,128)S(1)} %get-tuple-element.115, f32[202]{0:T(256)S(1)} %add_rsqrt_fusion.1, f32[202]{0:T(256)S(1)} %broadcast_multiply_fusion.5, f32[768]{0:T(1024)S(1)} %reshape.341, ...), kind=kOutput, calls=%fused_computation.41 | convolution fusion | flops 954549888 | bytes 7210144 | tf_op jit(solution)/shard_map/dot_general | solution.py:24
  111.1 0.8 reshape.323
  111.9 0.7 convert_element_type.288
  112.6 2.1 fusion.31
  114.7 1.1 convolution_convert_fusion.6
  115.8 1.4 convert_element_type.282
  117.2 1.4 convert_element_type.284
  118.6 1.4 convert_element_type.286
  120.0 2.4 reshape.348
  122.4 2.4 copy.122
  124.8 2.9 %fusion.32 = (bf16[12,64]{1,0:T(8,128)(2,1)}, bf16[2,101,12,64]{1,3,2,0:T(8,128)(2,1)}) fusion(bf16[2,101,12,64]{1,3,2,0:T(8,128)(2,1)} %copy.122, f32[2,12,101,101]{2,3,1,0:T(8,128)S(1)} %get-tuple-element.113, f32[2,12,101]{2,1,0:T(8,128)S(1)} %log_add_fusion), kind=kOutput, calls=%fused_computation.99 | convolution fusion | flops 32136624 | bytes 1611072 | tf_op jit(solution)/shard_map/bhqk,bqhd->bkhd/dot_general | solution.py:20
  127.8 1.4 convert_element_type.280
  129.1 2.2 copy.132
  131.3 2.0 reshape.327
  133.3 1.7 multiply_reduce_fusion
  135.3 0.7 copy-done.4
  137.8 1.0 reshape.326
  139.4 1.0 mul.187
  140.3 1.1 constant_dynamic-update-slice_fusion.2
  141.4 1.0 constant_dynamic-update-slice_fusion.1
  142.5 4.0 %multiply_reduce_fusion.2 = (bf16[768]{0:T(1024)(128)(2,1)S(1)}, f32[202]{0:T(256)S(1)}, f32[202]{0:T(256)S(1)}, bf16[768]{0:T(1024)(128)(2,1)S(1)}, f32[202,768]{1,0:T(8,128)S(1)}) fusion(f32[202,768]{1,0:T(8,128)S(1)} %reshape.335, f32[202]{0:T(256)S(1)} %copy-done.25, f32[202]{0:T(256)S(1)} %copy-done.27, f32[768]{0:T(1024)S(1)} %reshape.336, ...), kind=kOutput, calls=%fused_computation.42 | convolution fusion | flops 716260992 | bytes 5720224 | tf_op jit(solution)/shard_map/dot_general | solution.py:24
  146.5 1.0 add_convert_fusion.1
  147.5 1.1 reshape.328
  148.6 0.8 broadcast_select_fusion
  149.5 1.0 copy.136
  150.8 1.5 convolution_convert_fusion.3
  152.6 1.4 fusion.5
  154.0 1.6 copy.134
  155.6 1.0 copy.135
  156.6 4.5 %convolution_convert_fusion = bf16[768,2304]{1,0:T(8,128)(2,1)} fusion(bf16[202,2304]{0,1:T(8,128)(2,1)} %copy-done.8, f32[202,768]{1,0:T(8,128)S(1)} %reshape.335, f32[768]{0:T(1024)S(1)} %reshape.337, f32[202]{0:T(256)S(1)} %copy-done.26, f32[768]{0:T(1024)S(1)} %reshape.336, f32[202]{0:T(256)S(1)} %copy-done.28), kind=kOutput, calls=%fused_computation | convolution fusion | flops 717411840 | bytes 5098064 | tf_op jit(solution)/shard_map/dot_general | solution.py:28
  161.1 3.7 %convolution_convert_fusion.2 = bf16[768,3072]{1,0:T(8,128)(2,1)} fusion(bf16[202,3072]{1,0:T(8,128)(2,1)S(1)} %copy-done.15, f32[202,768]{1,0:T(8,128)S(1)} %get-tuple-element.115, f32[768]{0:T(1024)S(1)} %reshape.342, f32[768]{0:T(1024)S(1)} %reshape.341, f32[202]{0:T(256)S(1)} %copy-done.30, f32[202]{0:T(256)S(1)} %copy-done.24), kind=kOutput, calls=%fused_computation.2 | convolution fusion | flops 956290560 | bytes 6587984 | tf_op jit(solution)/shard_map/dot_general | solution.py:28
  164.8 3.6 %convolution_convert_fusion.1 = bf16[768,3072]{1,0:T(8,128)(2,1)} fusion(bf16[202,768]{1,0:T(8,128)(2,1)S(1)} %reshape.324, bf16[202,3072]{1,0:T(8,128)(2,1)S(1)} %copy-done.13), kind=kOutput, calls=%fused_computation.1 | convolution fusion | flops 955514880 | bytes 6269952 | tf_op jit(solution)/shard_map/dot_general | solution.py:28
  168.4 89.9 %shard_map.272 = (f32[24,2304]{1,0:T(8,128)}, f32[24,896]{1,0:T(8,128)}, f32[24,3072]{1,0:T(8,128)}, f32[24,3072]{1,0:T(8,128)}) custom-call(bf16[32,24,2304]{2,1,0:T(8,128)(2,1)} %bitcast.60, bf16[32,24,896]{2,1,0:T(8,128)(2,1)} %bitcast.61, bf16[32,24,3072]{2,1,0:T(8,128)(2,1)} %bitcast.58, bf16[32,24,3072]{2,1,0:T(8,128)(2,1)} %bitcast.59), custom_call_target="tpu_custom_call" | custom-call | tf_op jit(solution)/shard_map/pallas_call | solution.py:450
  258.3 0.7 slice.139
  259.0 0.6 slice.140
  259.6 0.8 fusion.34
  260.4 1.5 slice_bitcast_fusion
  261.9 0.6 slice.142
  262.5 0.6 slice.138
  263.1 0.6 slice.136
  263.7 0.6 slice.134
  264.3 0.6 slice.131
  264.9 0.6 slice.129
  265.5 0.6 slice.127
  266.7 1.6 copy.159
  268.3 1.7 copy.160
  270.0 0.7 copy.161
  (131 shorter events, 9.4 us)
Async XLA Ops:
  0.6 13.1 %copy-start = (bf16[2,101,768]{2,0,1:T(2,128)(2,1)S(1)}, bf16[2,101,768]{2,0,1:T(2,128)(2,1)}, u32[]{:S(2)}) copy-start(bf16[2,101,768]{2,0,1:T(2,128)(2,1)} %param.16) | copy-start | bytes 930820
  0.7 12.7 %copy-start.16 = (bf16[2,101,768]{2,0,1:T(2,128)(2,1)S(1)}, bf16[2,101,768]{2,0,1:T(2,128)(2,1)}, u32[]{:S(2)}) copy-start(bf16[2,101,768]{2,0,1:T(2,128)(2,1)} %param.17) | copy-start | bytes 930820
  1.4 12.3 %copy-start.31 = (pred[2]{0:T(512)(128)(4,1)}, pred[2]{0:T(512)(128)(4,1)S(1)}, u32[]{:S(2)}) copy-start(pred[2]{0:T(512)(128)(4,1)S(1)} %iota_compare_fusion.2) | copy-start | bytes 10
  89.2 3.0 %copy-start.3 = (bf16[2,101,12,64]{1,3,2,0:T(8,128)(2,1)}, bf16[2,101,12,64]{1,3,2,0:T(8,128)(2,1)S(1)}, u32[]{:S(2)}) copy-start(bf16[2,101,12,64]{1,3,2,0:T(8,128)(2,1)S(1)} %copy.115) | copy-start | bytes 930820
  92.2 2.0 copy-start.2
  95.1 2.1 copy-start.6
  97.3 10.6 %copy-start.23 = (f32[202]{0:T(256)}, f32[202]{0:T(256)S(1)}, u32[]{:S(2)}) copy-start(f32[202]{0:T(256)S(1)} %broadcast_multiply_fusion.5) | copy-start | bytes 2428
  97.5 10.4 %copy-start.29 = (f32[202]{0:T(256)}, f32[202]{0:T(256)S(1)}, u32[]{:S(2)}) copy-start(f32[202]{0:T(256)S(1)} %add_rsqrt_fusion.1) | copy-start | bytes 2428
  97.5 8.7 %slice-start.2 = ((s8[4718592]{0:T(1024)(128)(4,1)}), s8[4194304]{0:T(1024)(128)(4,1)S(1)}, s32[]{:S(2)}) async-start(s8[4718592]{0:T(1024)(128)(4,1)} %bitcast.75), calls=%async_computation.2 | async-start | bytes 8388608
  97.5 10.4 %slice-start = ((s8[4718592]{0:T(1024)(128)(4,1)}), s8[4194304]{0:T(1024)(128)(4,1)S(1)}, s32[]{:S(2)}) async-start(s8[4718592]{0:T(1024)(128)(4,1)} %bitcast.71), calls=%async_computation | async-start | bytes 8388608
  101.2 5.0 %copy-start.12 = (bf16[202,3072]{1,0:T(8,128)(2,1)}, bf16[202,3072]{1,0:T(8,128)(2,1)S(1)}, u32[]{:S(2)}) copy-start(bf16[202,3072]{1,0:T(8,128)(2,1)S(1)} %get-tuple-element.123) | copy-start | bytes 3723268
  101.2 5.0 %slice-start.3 = ((s8[4718592]{0:T(1024)(128)(4,1)}), s8[524288]{0:T(1024)(128)(4,1)S(1)}, s32[]{:S(2)}) async-start(s8[4718592]{0:T(1024)(128)(4,1)} %bitcast.75), calls=%async_computation.3 | async-start | bytes 1048576
  101.2 6.7 %slice-start.1 = ((s8[4718592]{0:T(1024)(128)(4,1)}), s8[524288]{0:T(1024)(128)(4,1)S(1)}, s32[]{:S(2)}) async-start(s8[4718592]{0:T(1024)(128)(4,1)} %bitcast.71), calls=%async_computation.1 | async-start | bytes 1048576
  106.2 1.7 copy-start.14
  112.6 2.1 copy-start.1
  135.0 1.0 copy-start.4
  136.0 1.0 copy-start.5
  140.3 2.1 copy-start.9
  140.3 2.2 copy-start.25
  140.3 2.2 copy-start.27
  142.5 4.0 %copy-start.8 = (bf16[202,2304]{0,1:T(8,128)(2,1)}, bf16[202,2304]{0,1:T(8,128)(2,1)S(1)}, u32[]{:S(2)}) copy-start(bf16[202,2304]{0,1:T(8,128)(2,1)S(1)} %constant_dynamic-update-slice_fusion) | copy-start | bytes 2792452
  146.5 2.1 copy-start.10
  146.5 2.1 copy-start.32
  147.5 3.2 %copy-start.18 = (bf16[32,96]{1,0:T(8,128)(2,1)S(1)}, bf16[32,96]{1,0:T(8,128)(2,1)}, u32[]{:S(2)}) copy-start(bf16[32,96]{1,0:T(8,128)(2,1)} %convert_element_type.288) | copy-start | bytes 18436
  147.5 3.2 %copy-start.19 = (bf16[32,24]{1,0:T(8,128)(2,1)S(1)}, bf16[32,24]{1,0:T(8,128)(2,1)}, u32[]{:S(2)}) copy-start(bf16[32,24]{1,0:T(8,128)(2,1)} %convert_element_type.282) | copy-start | bytes 4612
  147.5 3.2 %copy-start.20 = (bf16[32,24]{1,0:T(8,128)(2,1)S(1)}, bf16[32,24]{1,0:T(8,128)(2,1)}, u32[]{:S(2)}) copy-start(bf16[32,24]{1,0:T(8,128)(2,1)} %convert_element_type.284) | copy-start | bytes 4612
  147.5 3.2 %copy-start.21 = (bf16[32,24]{1,0:T(8,128)(2,1)S(1)}, bf16[32,24]{1,0:T(8,128)(2,1)}, u32[]{:S(2)}) copy-start(bf16[32,24]{1,0:T(8,128)(2,1)} %convert_element_type.286) | copy-start | bytes 4612
  147.5 3.2 %copy-start.22 = (bf16[32,24]{1,0:T(8,128)(2,1)S(1)}, bf16[32,24]{1,0:T(8,128)(2,1)}, u32[]{:S(2)}) copy-start(bf16[32,24]{1,0:T(8,128)(2,1)} %convert_element_type.280) | copy-start | bytes 4612
  147.5 3.3 %copy-start.7 = (bf16[202,768]{0,1:T(8,128)(2,1)S(1)}, bf16[202,768]{0,1:T(8,128)(2,1)}, u32[]{:S(2)}) copy-start(bf16[202,768]{0,1:T(8,128)(2,1)} %copy-done.6) | copy-start | bytes 930820
  154.0 1.6 copy-start.11
  154.0 2.6 copy-start.26
  154.0 2.6 copy-start.28
  156.6 4.5 %copy-start.15 = (bf16[202,3072]{1,0:T(8,128)(2,1)S(1)}, bf16[202,3072]{1,0:T(8,128)(2,1)}, u32[]{:S(2)}) copy-start(bf16[202,3072]{1,0:T(8,128)(2,1)} %copy-done.14) | copy-start | bytes 3723268
  156.6 4.5 %copy-start.24 = (f32[202]{0:T(256)S(1)}, f32[202]{0:T(256)}, u32[]{:S(2)}) copy-start(f32[202]{0:T(256)} %copy-done.23) | copy-start | bytes 2428
  156.6 4.5 %copy-start.30 = (f32[202]{0:T(256)S(1)}, f32[202]{0:T(256)}, u32[]{:S(2)}) copy-start(f32[202]{0:T(256)} %copy-done.29) | copy-start | bytes 2428
  161.1 3.7 %copy-start.13 = (bf16[202,3072]{1,0:T(8,128)(2,1)S(1)}, bf16[202,3072]{1,0:T(8,128)(2,1)}, u32[]{:S(2)}) copy-start(bf16[202,3072]{1,0:T(8,128)(2,1)} %copy-done.12) | copy-start | bytes 3723268
  258.2 11.7 %copy-start.17 = (f32[24,3072]{1,0:T(8,128)S(1)}, f32[24,3072]{1,0:T(8,128)}, u32[]{:S(2)}) copy-start(f32[24,3072]{1,0:T(8,128)} %get-tuple-element.30) | copy-start | bytes 884740
